TPU v7x, 1024 devices: a whole 4x4x32 slice. The times are simulated.
1024 devices in a mesh: fsdp: 128 (over z, x_lo, core), tp: 8 (over y, x_hi).
Axes of the slice: x: 4 (x_hi: 2, x_lo: 2; x = x_hi * 2 + x_lo), y: 4, z: 32, core: 2. Of those that a mesh axis runs over, the one named last changes fastest.
Arguments:
- momentum: float32 [128, 26624], P('fsdp', 'tp'), may hold values from -510 to 510
- gradient: float32 [128, 26624], P('fsdp', 'tp'), may hold values from -24 to 24
- basis: float32 [8, 26624], P(None, 'tp'), may hold values from -0.0390625 to 0.0390625
- weight: bfloat16 [128, 26624], P('fsdp', 'tp'), may hold values from -0.5 to 0.5
- inputs: bfloat16 [16384, 128], P('fsdp'), may hold values from -6 to 6
Outputs:
- new_momentum: float32 [128, 26624], P('fsdp', 'tp')
- new_basis: float32 [8, 26624], P(None, 'tp')
- new_weight: bfloat16 [128, 26624], P('fsdp', 'tp')
- activations: bfloat16 [16384, 26624], P('fsdp', 'tp')
All inputs are finite; a program needn't handle non-finite values.
Results may differ from a plain program's by a relative error of at most 0.0049.
Values may be sent and summed in bfloat16 or wider, within the bound.
No kernel may reach another device: no remote copies, remote signals or barrier semaphores. Data moves between devices by JAX's collectives and lax.ppermute only.
A program may use at most 32 MiB of HBM per device.

v0:
```python
import math

import jax
import jax.numpy as jnp
from jax import lax
from jax.sharding import PartitionSpec as P

decay_rate = 0.8
step_size = 0.5
epsilon = 1e-06
highest = lax.Precision.HIGHEST


def product(left, right):
    return jnp.dot(left, right, precision=highest, preferred_element_type=jnp.float32)


def contract_rows(left, right):
    return lax.dot_general(
        left, right, (((0,), (0,)), ((), ())), precision=highest, preferred_element_type=jnp.float32
    )


def contract_cols(left, right):
    return lax.dot_general(
        left, right, (((1,), (1,)), ((), ())), precision=highest, preferred_element_type=jnp.float32
    )


def lower_solve(lower, right):
    return lax.linalg.triangular_solve(lower, right, left_side=True, lower=True)


def on_device(momentum, gradient, basis, weight, inputs):
    fsdp_size = lax.axis_size("fsdp")
    tp_size = lax.axis_size("tp")
    rows_local = momentum.shape[0]
    width_local = momentum.shape[1]
    scale = step_size * math.sqrt(width_local * tp_size / (rows_local * fsdp_size))
    buffer = decay_rate * momentum + gradient
    partial_power = contract_cols(buffer, basis)
    power = lax.psum(partial_power, "tp")
    gram, raw_coeff = lax.psum((contract_rows(power, power), contract_rows(power, buffer)), "fsdp")
    lower = jnp.linalg.cholesky(gram)
    ortho = lower_solve(lower, power.T).T
    coeff = lower_solve(lower, raw_coeff)
    squares = lax.psum(jnp.sum(coeff * coeff, axis=1), "tp")
    new_basis = coeff / jnp.sqrt(squares + epsilon)[:, None]
    new_momentum = buffer - (1.0 - decay_rate) * product(ortho, coeff)
    new_weight = (weight.astype(jnp.float32) - scale * product(ortho, new_basis)).astype(
        jnp.bfloat16
    )
    summed = jnp.dot(
        inputs,
        lax.all_gather(new_weight, "fsdp", axis=0, tiled=True),
        preferred_element_type=jnp.float32,
    )
    activations = summed.astype(jnp.bfloat16)
    return (new_momentum, new_basis, new_weight, activations)


def solution(mesh):
    return jax.shard_map(
        on_device,
        mesh=mesh,
        in_specs=(
            P("fsdp", "tp"),
            P("fsdp", "tp"),
            P(None, "tp"),
            P("fsdp", "tp"),
            P("fsdp", None),
        ),
        out_specs=(P("fsdp", "tp"), P(None, "tp"), P("fsdp", "tp"), P("fsdp", "tp")),
        check_vma=False,
    )
```

profile of v0, /device:TPU:1, one launch (start us, length us, event | category | flops | bytes accessed | tf_op | source)
XLA Modules:
  0.0 942.7 jit_solution(10891407149952480822)
XLA Ops:
  7.2 0.8 copy-done
  8.1 1.0 convolution_bitcast_fusion
  9.1 0.8 fusion.10
  9.9 21.6 %psum.28 = f32[8]{0:T(128)S(1)} all-reduce(f32[8]{0:T(128)S(1)} %convolution_bitcast_fusion), channel_id=1, replica_groups=mesh['fsdp'=128,'tp'=8] {'tp'}, use_global_device_ids=true, to_apply=%region_0.0 | all-reduce | flops 8 | bytes 64 | tf_op jit(solution)/shard_map/psum | solution.py:42
  31.5 0.7 broadcast_multiply_fusion
  32.2 0.1 broadcast_multiply_fusion.3
  32.3 225.0 %psum.29 = f32[8,8]{0,1:T(8,128)S(1)} all-reduce(f32[8,8]{0,1:T(8,128)S(1)} %broadcast_multiply_fusion.3), channel_id=1, replica_groups=mesh['fsdp'=128,'tp'=8] {'fsdp'}, use_global_device_ids=true, to_apply=%region_1.0 | all-reduce | flops 64 | bytes 512 | tf_op jit(solution)/shard_map/psum | solution.py:43
  257.3 0.1 copy.15
  257.4 0.7 cholesky.16
  258.1 0.6 compare_reduce_fusion
  258.8 0.6 fusion.4
  259.4 0.6 custom-call.8
  260.0 0.1 convolution_bitcast_fusion.1
  260.2 523.7 %all-reduce.2.cloned.1.call-done = f32[8,3328]{1,0:T(8,128)} async-done(((f32[8,3328]{1,0:T(8,128)}), f32[8,3328]{1,0:T(8,128)}) %all-reduce.2.cloned.1.call-update) | async-done | bytes 106512 | tf_op jit(solution)/shard_map/psum | solution.py:43
  783.9 1.3 multiply_reduce_fusion
  785.2 18.8 %psum.31 = f32[8]{0:T(128)S(1)} all-reduce(f32[8]{0:T(128)S(1)} %get-tuple-element.16), channel_id=1, replica_groups=mesh['fsdp'=128,'tp'=8] {'tp'}, use_global_device_ids=true, to_apply=%region_6.7 | all-reduce | flops 8 | bytes 64 | tf_op jit(solution)/shard_map/psum | solution.py:47
  803.9 0.3 convolution_reduce_fusion.1
  804.2 0.1 broadcast_divide_fusion
  804.3 1.4 reshape_subtract_fusion
  805.7 0.3 convolution_reduce_fusion
  806.0 0.7 subtract_convert_fusion
  806.7 127.5 %all-gather = bf16[128,1,3328]{2,1,0:T(2,128)(2,1)S(1)} all-gather(bf16[1,1,3328]{2,1,0:T(2,128)(2,1)S(1)} %bitcast.40), channel_id=1, replica_groups=mesh['fsdp'=128,'tp'=8] {'fsdp'}, dimensions={0}, use_global_device_ids=true | all-gather | bytes 858624 | tf_op jit(solution)/shard_map/all_gather | solution.py:55
  934.2 0.4 fusion
  934.6 1.3 copy.17
  (14 shorter events, 0.2 us)
Async XLA Ops:
  7.2 0.9 copy-start
  7.2 927.0 %copy-start.3 = (bf16[128,128]{1,0:T(8,128)(2,1)S(1)}, bf16[128,128]{1,0:T(8,128)(2,1)}, u32[]{:S(2)}) copy-start(bf16[128,128]{1,0:T(8,128)(2,1)} %param.9) | copy-start | bytes 98308
  7.2 776.7 %all-reduce.2.cloned.1.call-start = ((), (), s32[]{:S(2)}) async-start(), calls=%async_computation | async-start | bytes 212992 | tf_op jit(solution)/shard_map/psum | solution.py:43
  804.3 130.3 %copy-start.1 = (f32[8,3328]{1,0:T(8,128)}, f32[8,3328]{1,0:T(8,128)S(1)}, u32[]{:S(2)}) copy-start(f32[8,3328]{1,0:T(8,128)S(1)} %broadcast_divide_fusion) | copy-start | bytes 319492
  806.7 127.9 %copy-start.2 = (bf16[1,3328]{1,0:T(2,128)(2,1)}, bf16[1,3328]{1,0:T(2,128)(2,1)S(1)}, u32[]{:S(2)}) copy-start(bf16[1,3328]{1,0:T(2,128)(2,1)S(1)} %subtract_convert_fusion) | copy-start | bytes 19972
Sparse Core Ops, SparseCore 0:
  32.3 751.4 all-reduce.1
where the time goes:
time: 943 us
  waiting for transfers between devices  524 us (56%)
  blocking collectives  393 us (42%)
  between operations  14.1 us (1%)
    psum x1, waiting for transfers between devices, on_device(): lax.psum((contract_rows(power, power), contract_rows(power, buffer)), 'fs...  524 us
    psum x1, blocking collectives, on_device(): lax.psum((contract_rows(power, power), contract_rows(power, buffer)), 'fs...  225 us
    all_gather x1, blocking collectives, on_device(): lax.all_gather(new_weight, 'fsdp', axis=0, tiled=True)  127 us
    psum x1, blocking collectives, on_device(): power = lax.psum(partial_power, 'tp')  21.6 us
  transfers between devices with their start and end apart: 1, of which 1 were waited for; matrix products, arithmetic and copies ran while one was open for 0% of the time, Pallas kernels for 0%

commit v1 on v0

v1 whole, which is shorter than its diff:
```python
import math

import jax
import jax.numpy as jnp
from jax import lax
from jax.sharding import Mesh, PartitionSpec as P

decay_rate = 0.8
step_size = 0.5
epsilon = 1e-06
highest = lax.Precision.HIGHEST
rows_axes = ("zh", "zl", "a")


def product(left, right):
    return jnp.dot(left, right, precision=highest, preferred_element_type=jnp.float32)


def contract_cols(left, right):
    return lax.dot_general(
        left, right, (((1,), (1,)), ((), ())), precision=highest, preferred_element_type=jnp.float32
    )


def lower_solve(lower, right):
    return lax.linalg.triangular_solve(lower, right, left_side=True, lower=True)


def spread(block, axes):
    size = lax.axis_size(axes)
    return lax.all_to_all(jnp.broadcast_to(block[None], (size,) + block.shape), axes, 0, 0)


def on_device(momentum, gradient, basis, weight, inputs):
    zh, zl, a = (lax.axis_size(n) for n in rows_axes)
    rows = zh * zl * a
    width_local = momentum.shape[1]
    rank = basis.shape[0]
    scale = step_size * math.sqrt(width_local * lax.axis_size("tp") / rows)
    buffer = decay_rate * momentum + gradient
    partial_power = contract_cols(buffer, basis)
    power_row = jnp.sum(spread(partial_power, "tp"), axis=0)
    high = lax.reduce_precision(power_row, 8, 7)
    middle = lax.reduce_precision(power_row - high, 8, 7)
    low = power_row - high - middle
    tail = jnp.concatenate([high, middle, low, jnp.zeros((1, 128 - 3 * rank))], axis=1).astype(jnp.bfloat16)
    upper = jnp.concatenate([buffer.astype(jnp.bfloat16), tail], axis=1)
    under = jnp.concatenate([weight, jnp.zeros_like(tail)], axis=1)
    far = spread(jnp.concatenate([upper, under], axis=0), "zh")
    near = spread(far, "zl").reshape(zl * zh, 2, width_local + 128)
    upper_rows = lax.all_gather(near[:, 0, :], "a", axis=0, tiled=True)
    weight_rows = lax.all_gather(near[:, 1, :width_local], "a", axis=0, tiled=True)
    buffer_rows = upper_rows[:, :width_local]
    parts = upper_rows[:, width_local : width_local + 3 * rank].astype(jnp.float32)
    power = (parts[:, :rank] + parts[:, rank : 2 * rank] + parts[:, 2 * rank :]).T
    gram = contract_cols(power, power)
    lower = jnp.linalg.cholesky(gram)
    ortho = lower_solve(lower, power)
    coeff = product(ortho, buffer_rows.astype(jnp.float32))
    local_squares = jnp.sum(coeff * coeff, axis=1)
    squares = jnp.sum(spread(local_squares[None], "tp"), axis=(0, 1))
    new_basis = coeff / jnp.sqrt(squares + epsilon)[:, None]
    place = (lax.axis_index("a") * zl + lax.axis_index("zl")) * zh + lax.axis_index("zh")
    own = lax.dynamic_slice(ortho, (0, place), (8, 1))
    new_momentum = buffer - (1.0 - decay_rate) * product(own.T, coeff)
    step = lax.dot_general(
        ortho, new_basis, (((0,), (0,)), ((), ())), precision=highest, preferred_element_type=jnp.float32
    )
    new_rows = (weight_rows.astype(jnp.float32) - scale * step).astype(jnp.bfloat16)
    new_weight = lax.dynamic_slice(new_rows, (place, 0), (1, width_local))
    ordered = inputs.reshape(-1, zh, zl, a).transpose(0, 3, 2, 1).reshape(-1, rows)
    summed = jnp.dot(ordered, new_rows, preferred_element_type=jnp.float32)
    return (new_momentum, new_basis, new_weight, summed.astype(jnp.bfloat16))


def solution(mesh):
    fsdp, tp = mesh.devices.shape
    fine = Mesh(mesh.devices.reshape(fsdp // 16, 4, 4, tp), rows_axes + ("tp",))
    return jax.shard_map(
        on_device,
        mesh=fine,
        in_specs=(
            P(rows_axes, "tp"),
            P(rows_axes, "tp"),
            P(None, "tp"),
            P(rows_axes, "tp"),
            P(rows_axes, None),
        ),
        out_specs=(P(rows_axes, "tp"), P(None, "tp"), P(rows_axes, "tp"), P(rows_axes, "tp")),
        check_vma=False,
    )
```

time: 943 us -> 120 us (0.13)
  waiting for transfers between devices: 524 us -> 13.9 us
  blocking collectives: 393 us -> 74.3 us
  starting transfers between devices: 0.04 us -> 15.6 us
  between operations: 14.1 us -> 0.8 us
    psum x1 -> x0, waiting for transfers between devices: 524 us -> none  [on_device(): lax.psum((contract_rows(power, power), contract_rows(power, buffer)), 'fs...]
    psum x3 -> x0, blocking collectives: 265 us -> none  [the longest x1 225 us: on_device(): lax.psum((contract_rows(power, power), contract_rows(power, buffer)), 'fs...]
    all_gather x1 -> x2, blocking collectives: 127 us -> 22.9 us  [the longest x1 13.8 us: on_device(): upper_rows = lax.all_gather(near[:, 0, :], 'a', axis=0, tiled=True)]
    all_to_all x0 -> x1, blocking collectives: none -> 51.5 us  [spread(): lax.all_to_all(jnp.broadcast_to(block[None], (size,) + block.shape), axes...]
    all_to_all x0 -> x3, starting transfers between devices: none -> 15.6 us  [spread(): lax.all_to_all(jnp.broadcast_to(block[None], (size,) + block.shape), axes...]
    all_to_all x0 -> x3, waiting for transfers between devices: none -> 13.9 us  [spread(): lax.all_to_all(jnp.broadcast_to(block[None], (size,) + block.shape), axes...]
  transfers between devices with their start and end apart: 1 -> 3, of which waited for: 1 -> 2; matrix products, arithmetic and copies ran while one was open for 0% -> 1% of each run, Pallas kernels for 0% -> 0%
where the time goes in v1:
time: 120 us
  blocking collectives  74.3 us (62%)
  starting transfers between devices  15.6 us (13%)
  waiting for transfers between devices  13.9 us (12%)
  local copies, waits for them, and re-layouts  5.47 us (5%)
  other arithmetic  4.98 us (4%)
  matrix products  4.44 us (4%)
    all_to_all x1, blocking collectives, spread(): lax.all_to_all(jnp.broadcast_to(block[None], (size,) + block.shape), axes...  51.5 us
    all_to_all x3, starting transfers between devices, spread(): lax.all_to_all(jnp.broadcast_to(block[None], (size,) + block.shape), axes...  15.6 us
    all_to_all x3, waiting for transfers between devices, spread(): lax.all_to_all(jnp.broadcast_to(block[None], (size,) + block.shape), axes...  13.9 us
    all_gather x1, blocking collectives, on_device(): upper_rows = lax.all_gather(near[:, 0, :], 'a', axis=0, tiled=True)  13.8 us
    all_gather x1, blocking collectives, on_device(): lax.all_gather(near[:, 1, :width_local], 'a', axis=0, tiled=True)  9.06 us
  transfers between devices with their start and end apart: 3, of which 2 were waited for; matrix products, arithmetic and copies ran while one was open for 1% of the time, Pallas kernels for 0%

profile of v1, /device:TPU:1, one launch (start us, length us, event | category | flops | bytes accessed | tf_op | source)
XLA Modules:
  0.0 119.6 jit_solution(15609095186616544607)
XLA Ops:
  0.6 0.9 copy-done
  1.5 1.0 convolution_bitcast_fusion
  2.5 0.7 broadcast_in_dim.11
  3.2 7.5 %all-to-all-start = ((f32[8,1,8]{2,1,0:T(1,128)}), f32[8,1,8]{2,1,0:T(1,128)S(1)}, u32[]{:S(2)}, u32[]{:S(2)}) async-start(f32[8,1,8]{2,1,0:T(1,128)} %broadcast_in_dim.11), calls=%async_computation | async-start | bytes 8192 | tf_op jit(solution)/shard_map/all_to_all | solution.py:31
  10.7 0.7 fusion.17
  11.4 5.7 %all-to-all-done = f32[8,1,8]{2,1,0:T(1,128)S(1)} async-done(((f32[8,1,8]{2,1,0:T(1,128)}), f32[8,1,8]{2,1,0:T(1,128)S(1)}, u32[]{:S(2)}, u32[]{:S(2)}) %all-to-all-start) | async-done | bytes 288 | tf_op jit(solution)/shard_map/all_to_all | solution.py:31
  17.3 0.7 fusion.5
  18.1 51.5 %all_to_all.20 = bf16[8,2,3456]{2,1,0:T(2,128)(2,1)S(1)} all-to-all(bf16[8,2,3456]{2,1,0:T(2,128)(2,1)S(1)} %broadcast_in_dim.13), channel_id=1, replica_groups=mesh['zh'=8,'zl'=4,'a'=4,'tp'=8] {'zh'}, dimensions={0} | all-to-all | bytes 221184 | tf_op jit(solution)/shard_map/all_to_all | solution.py:31
  69.6 0.8 broadcast_in_dim.14
  70.3 4.9 %all-to-all-start.2 = ((bf16[4,8,2,3456]{3,1,2,0:T(8,128)(2,1)}), bf16[4,8,2,3456]{3,1,2,0:T(8,128)(2,1)S(1)}, u32[]{:S(2)}, u32[]{:S(2)}) async-start(bf16[4,8,2,3456]{3,1,2,0:T(8,128)(2,1)} %broadcast_in_dim.14), calls=%async_computation.2 | async-start | bytes 884736 | tf_op jit(solution)/shard_map/all_to_all | solution.py:31
  75.3 8.2 %all-to-all-done.2 = bf16[4,8,2,3456]{3,1,2,0:T(8,128)(2,1)S(1)} async-done(((bf16[4,8,2,3456]{3,1,2,0:T(8,128)(2,1)}), bf16[4,8,2,3456]{3,1,2,0:T(8,128)(2,1)S(1)}, u32[]{:S(2)}, u32[]{:S(2)}) %all-to-all-start.2) | async-done | bytes 442400 | tf_op jit(solution)/shard_map/all_to_all | solution.py:31
  83.6 13.8 %all-gather = bf16[128,1,3456]{2,0,1:T(8,128)(2,1)S(1)} all-gather(bf16[32,1,3456]{2,0,1:T(8,128)(2,1)S(1)} %slice.38), channel_id=2, replica_groups=mesh['zh'=8,'zl'=4,'a'=4,'tp'=8] {'a'}, dimensions={0}, use_global_device_ids=true | all-gather | bytes 1105920 | tf_op jit(solution)/shard_map/all_gather | solution.py:51
  97.9 0.7 cholesky.16
  98.6 0.6 compare_reduce_fusion
  99.3 0.6 fusion.7
  100.0 0.6 custom-call.6
  100.8 0.6 multiply_reduce_fusion
  101.9 0.6 reshape_subtract_fusion
  102.6 0.6 broadcast_in_dim.16
  103.2 3.3 %all-to-all-start.3 = ((f32[8,1,8]{2,1,0:T(1,128)}), f32[8,1,8]{2,1,0:T(1,128)S(1)}, u32[]{:S(2)}, u32[]{:S(2)}) async-start(f32[8,1,8]{2,1,0:T(1,128)} %broadcast_in_dim.16), calls=%async_computation.3 | async-start | bytes 8192 | tf_op jit(solution)/shard_map/all_to_all | solution.py:31
  106.5 9.1 %all-gather.1 = bf16[128,1,3328]{2,0,1:T(8,128)(2,1)S(1)} all-gather(bf16[32,1,3328]{2,0,1:T(8,128)(2,1)S(1)} %slice.44), channel_id=3, replica_groups=mesh['zh'=8,'zl'=4,'a'=4,'tp'=8] {'a'}, dimensions={0}, use_global_device_ids=true | all-gather | bytes 1064960 | tf_op jit(solution)/shard_map/all_gather | solution.py:52
  115.7 1.6 %fusion.1 = bf16[128,3328]{1,0:T(8,128)(2,1)S(1)} fusion(f32[8,128]{1,0:T(8,128)S(1)} %fusion.8, f32[8,3328]{1,0:T(8,128)S(1)} %broadcast_divide_fusion, bf16[128,1,3328]{2,0,1:T(8,128)(2,1)S(1)} %all-gather.1), kind=kOutput, calls=%fused_computation.2 | convolution fusion | flops 42598400 | bytes 1814528 | tf_op jit(solution)/shard_map/dot_general | solution.py:66
  117.3 0.6 constant_dynamic-slice_fusion
  118.3 1.3 %copy.39 = bf16[128,3328]{1,0:T(8,128)(2,1)} copy(bf16[128,3328]{0,1:T(8,128)(2,1)S(1)} %fusion.2) | data formatting | bytes 1703936
  (34 shorter events, 2.1 us)
Async XLA Ops:
  0.6 0.9 copy-start
  3.2 13.9 %all-to-all-start = ((f32[8,1,8]{2,1,0:T(1,128)}), f32[8,1,8]{2,1,0:T(1,128)S(1)}, u32[]{:S(2)}, u32[]{:S(2)}) async-start(f32[8,1,8]{2,1,0:T(1,128)} %broadcast_in_dim.11), calls=%async_computation | async-start | bytes 8192 | tf_op jit(solution)/shard_map/all_to_all | solution.py:31
  69.5 5.7 %copy-start.4 = (bf16[128,128]{1,0:T(8,128)(2,1)S(1)}, bf16[128,128]{1,0:T(8,128)(2,1)}, u32[]{:S(2)}) copy-start(bf16[128,128]{1,0:T(8,128)(2,1)} %param.9) | copy-start | bytes 98308
  70.3 13.2 %all-to-all-start.2 = ((bf16[4,8,2,3456]{3,1,2,0:T(8,128)(2,1)}), bf16[4,8,2,3456]{3,1,2,0:T(8,128)(2,1)S(1)}, u32[]{:S(2)}, u32[]{:S(2)}) async-start(bf16[4,8,2,3456]{3,1,2,0:T(8,128)(2,1)} %broadcast_in_dim.14), calls=%async_computation.2 | async-start | bytes 884736 | tf_op jit(solution)/shard_map/all_to_all | solution.py:31
  97.5 4.5 %copy-start.2 = (f32[1,3328]{1,0:T(1,128)S(1)}, f32[1,3328]{1,0:T(1,128)}, u32[]{:S(2)}) copy-start(f32[1,3328]{1,0:T(1,128)} %param.6) | copy-start | bytes 39940
  97.5 4.5 %copy-start.3 = (f32[1,3328]{1,0:T(1,128)S(1)}, f32[1,3328]{1,0:T(1,128)}, u32[]{:S(2)}) copy-start(f32[1,3328]{1,0:T(1,128)} %param.5) | copy-start | bytes 39940
  103.2 12.4 %all-to-all-start.3 = ((f32[8,1,8]{2,1,0:T(1,128)}), f32[8,1,8]{2,1,0:T(1,128)S(1)}, u32[]{:S(2)}, u32[]{:S(2)}) async-start(f32[8,1,8]{2,1,0:T(1,128)} %broadcast_in_dim.16), calls=%async_computation.3 | async-start | bytes 8192 | tf_op jit(solution)/shard_map/all_to_all | solution.py:31
  115.7 1.6 %copy-start.1 = (f32[8,3328]{1,0:T(8,128)}, f32[8,3328]{1,0:T(8,128)S(1)}, u32[]{:S(2)}) copy-start(f32[8,3328]{1,0:T(8,128)S(1)} %broadcast_divide_fusion) | copy-start | bytes 319492

commit v2 on v1

v2 whole, which is shorter than its diff:
```python
import functools
import math

import jax
import jax.numpy as jnp
from jax import lax
from jax.experimental import pallas as pl
from jax.experimental.pallas import tpu as pltpu
from jax.sharding import Mesh, PartitionSpec as P

decay_rate = 0.8
step_size = 0.5
epsilon = 1e-06
highest = lax.Precision.HIGHEST
rows_axes = ("zh", "zl", "a")
tail = 128
bf16 = jnp.bfloat16
f32 = jnp.float32


def spread(blocks, axes):
    return lax.all_to_all(blocks, axes, 0, 0)


def replicated(block, axes):
    return jnp.broadcast_to(block[None], (lax.axis_size(axes),) + block.shape)


def iota(shape, dim):
    return lax.broadcasted_iota(jnp.int32, shape, dim)


def three_parts(x):
    high = x.astype(bf16).astype(f32)
    middle = (x - high).astype(bf16).astype(f32)
    return high, middle, x - high - middle


def first_kernel(momentum, gradient, basis, weight, out):
    width = momentum.shape[1]
    rank = basis.shape[0]
    total = jnp.zeros((rank, 128), f32)
    pieces = []
    for start in range(0, width, 128):
        cut = slice(start, start + 128)
        buffer = decay_rate * momentum[:, cut] + gradient[:, cut]
        pieces.append(buffer)
        total = total + basis[:, cut] * buffer
    sums = jnp.broadcast_to(jnp.sum(total, axis=1, keepdims=True), (rank, 128))
    lane, sub = iota((rank, 128), 1), iota((rank, 128), 0)
    row = jnp.sum(jnp.where(lane % rank == sub, sums, 0.0), axis=0, keepdims=True)
    high, middle, low = three_parts(row)
    place = iota((1, 128), 1)
    coded = jnp.where(place < rank, high, jnp.where(place < 2 * rank, middle, jnp.where(place < 3 * rank, low, 0.0)))
    upper = jnp.concatenate(pieces + [coded], axis=1).astype(bf16)
    under = jnp.concatenate([weight[...], jnp.zeros((1, tail), bf16)], axis=1)
    both = jnp.concatenate([upper, under], axis=0)
    for peer in range(out.shape[0]):
        out[peer] = both


def second_kernel(upper_rows, out):
    rows = upper_rows.shape[0]
    width = upper_rows.shape[1] - tail
    rank = out.shape[1] - rows
    buffer = upper_rows[:, :width]
    square = lax.dot_general(buffer, buffer, (((1,), (1,)), ((), ())), preferred_element_type=f32)
    coded = upper_rows[:, width:].astype(f32).T
    power = coded[:rank] + coded[rank : 2 * rank] + coded[2 * rank : 3 * rank]
    for peer in range(out.shape[0]):
        out[peer, :rows] = square
        out[peer, rows:] = power


def third_kernel(
    scale, place, sums, upper_rows, weight_rows, momentum, gradient, inputs, new_momentum, new_basis, new_weight, activations
):
    rows, width = weight_rows.shape
    rank = new_basis.shape[0]
    total = sums[0]
    for peer in range(1, sums.shape[0]):
        total = total + sums[peer]
    square, power = total[:rows], total[rows:]
    gram = lax.dot_general(power, power, (((1,), (1,)), ((), ())), precision=highest, preferred_element_type=f32)
    sub = iota((rank, rows), 0)
    left = jnp.concatenate([gram, jnp.zeros((rank, rows - rank), f32)], axis=1)
    ortho = power
    for k in range(rank):
        column = jnp.broadcast_to(left[:, k : k + 1], (rank, rows))
        pivot = jnp.broadcast_to(column[k : k + 1], (rank, rows))
        root = 1.0 / jnp.sqrt(pivot)
        left_row = left[k : k + 1] * root
        ortho_row = ortho[k : k + 1] * root
        factor = column * root
        left = jnp.where(sub > k, left - factor * left_row, left)
        ortho = jnp.where(sub > k, ortho - factor * ortho_row, jnp.where(sub == k, ortho_row, ortho))
    along = lax.dot_general(ortho, square, (((1,), (0,)), ((), ())), precision=highest, preferred_element_type=f32)
    squares = jnp.maximum(jnp.sum(along * ortho, axis=1, keepdims=True), 0.0)
    inverse = 1.0 / jnp.sqrt(squares + epsilon)
    high, middle, low = three_parts(ortho)
    stacked = jnp.concatenate([high, middle, low], axis=0).astype(bf16)
    right_side = jnp.concatenate([high, high, middle, middle, high, low], axis=0)
    turned = jnp.concatenate([right_side, jnp.zeros((rows - 6 * rank, rows), f32)], axis=0).T.astype(bf16)
    here = place[0]
    own = jnp.sum(jnp.where(iota((rank, rows), 1) == here, ortho, 0.0), axis=1, keepdims=True) * (1.0 - decay_rate)
    chosen = (iota((16, rows), 1) == here).astype(f32).astype(bf16)
    left_side = jnp.concatenate([inputs[...], chosen], axis=0)
    chunk = 256
    for start in range(0, width, chunk):
        cut = slice(start, start + chunk)
        parts = jnp.dot(stacked, upper_rows[:, cut], preferred_element_type=f32)
        coeff = parts[:rank] + parts[rank : 2 * rank] + parts[2 * rank :]
        buffer = decay_rate * momentum[:, cut] + gradient[:, cut]
        new_momentum[:, cut] = buffer - jnp.sum(own * coeff, axis=0, keepdims=True)
        basis = coeff * inverse
        new_basis[:, cut] = basis
        high, middle, low = three_parts(basis)
        under = jnp.concatenate([high, middle, high, middle, low, high], axis=0).astype(bf16)
        step = jnp.dot(turned[:, : 6 * rank], under, preferred_element_type=f32)
        fresh = (weight_rows[:, cut].astype(f32) - scale * step).astype(bf16)
        result = jnp.dot(left_side, fresh, preferred_element_type=f32).astype(bf16)
        activations[:, cut] = result[: inputs.shape[0]]
        new_weight[:, cut] = result[inputs.shape[0] : inputs.shape[0] + 1]


vmem = pl.BlockSpec(memory_space=pltpu.VMEM)


def first_call(peers, momentum, gradient, basis, weight):
    return pl.pallas_call(
        first_kernel,
        out_shape=jax.ShapeDtypeStruct((peers, 2, momentum.shape[1] + tail), bf16),
        in_specs=[vmem] * 4,
        out_specs=vmem,
        name="first",
    )(momentum, gradient, basis, weight)


def second_call(peers, rank, upper_rows):
    rows = upper_rows.shape[0]
    return pl.pallas_call(
        second_kernel,
        out_shape=jax.ShapeDtypeStruct((peers, rows + rank, rows), f32),
        in_specs=[vmem],
        out_specs=vmem,
        name="second",
    )(upper_rows)


def third_call(scale, rank, place, sums, upper_rows, weight_rows, momentum, gradient, inputs):
    width = weight_rows.shape[1]
    return pl.pallas_call(
        functools.partial(third_kernel, scale),
        out_shape=(
            jax.ShapeDtypeStruct((1, width), f32),
            jax.ShapeDtypeStruct((rank, width), f32),
            jax.ShapeDtypeStruct((1, width), bf16),
            jax.ShapeDtypeStruct((inputs.shape[0], width), bf16),
        ),
        in_specs=[pl.BlockSpec(memory_space=pltpu.SMEM)] + [vmem] * 6,
        out_specs=(vmem,) * 4,
        name="third",
    )(place, sums, upper_rows, weight_rows, momentum, gradient, inputs)


def on_device(momentum, gradient, basis, weight, inputs):
    zh, zl, a = (lax.axis_size(n) for n in rows_axes)
    rows = zh * zl * a
    width = momentum.shape[1]
    rank = basis.shape[0]
    peers = lax.axis_size("tp")
    scale = step_size * math.sqrt(width * peers / rows)
    far = spread(first_call(zh, momentum, gradient, basis, weight), "zh")
    near = spread(replicated(far, "zl"), "zl").reshape(zl * zh, 2, width + tail)
    upper_rows = lax.all_gather(near[:, 0, :], "a", axis=0, tiled=True)
    weight_rows = lax.all_gather(near[:, 1, :width], "a", axis=0, tiled=True)
    sums = spread(second_call(peers, rank, upper_rows), "tp")
    place = (lax.axis_index("a") * zl + lax.axis_index("zl")) * zh + lax.axis_index("zh")
    ordered = inputs.reshape(-1, zh, zl, a).transpose(0, 3, 2, 1).reshape(-1, rows)
    return third_call(
        scale, rank, place.reshape(1).astype(jnp.int32), sums, upper_rows, weight_rows, momentum, gradient, ordered
    )


def solution(mesh):
    fsdp, tp = mesh.devices.shape
    fine = Mesh(mesh.devices.reshape(fsdp // 16, 4, 4, tp), rows_axes + ("tp",))
    return jax.shard_map(
        on_device,
        mesh=fine,
        in_specs=(
            P(rows_axes, "tp"),
            P(rows_axes, "tp"),
            P(None, "tp"),
            P(rows_axes, "tp"),
            P(rows_axes, None),
        ),
        out_specs=(P(rows_axes, "tp"), P(None, "tp"), P(rows_axes, "tp"), P(rows_axes, "tp")),
        check_vma=False,
    )
```

time: 120 us -> 114 us (0.950)
  blocking collectives: 74.3 us -> 94.4 us
  waiting for transfers between devices: 13.9 us -> 0.01 us
  Pallas kernels: 0 us -> 10.5 us
  starting transfers between devices: 15.6 us -> 6.49 us
  other arithmetic: 4.98 us -> 0 us
  matrix products: 4.44 us -> 0 us
  local copies, waits for them, and re-layouts: 5.47 us -> 1.77 us
    all_to_all x1 -> x2, blocking collectives: 51.5 us -> 69.6 us  [spread(): return lax.all_to_all(blocks, axes, 0, 0)]
    all_to_all x3 -> x1, waiting for transfers between devices: 13.9 us -> 0.01 us  [spread(): return lax.all_to_all(blocks, axes, 0, 0)]
    pallas_call x0 -> x3, Pallas kernels: none -> 10.5 us  [the longest x1 6.44 us: third_call(): pl.pallas_call(functools.partial(third_kernel, scale), out_shape=(jax.Sha...]
    all_to_all x3 -> x1, starting transfers between devices: 15.6 us -> 6.49 us  [spread(): return lax.all_to_all(blocks, axes, 0, 0)]
    dot_general x6 -> x0, matrix products: 4.18 us -> none  [the longest x1 1.59 us: on_device(): lax.dot_general(ortho, new_basis, (((0,), (0,)), ((), ())), precision=hig...]
    all_gather x1, blocking collectives: 9.06 us -> 12.6 us  [on_device(): weight_rows = lax.all_gather(near[:, 1, :width], 'a', axis=0, tiled=True)]
    another operation x5 -> x0, other arithmetic: 2.7 us -> none  [the longest x3 1.43 us: on_device(): lower = jnp.linalg.cholesky(gram)]
    broadcast_in_dim x5 -> x1, local copies, waits for them, and re-layouts: 2.11 us -> 0.03 us  [replicated(): return jnp.broadcast_to(block[None], (lax.axis_size(axes),) + block.shape)]
  transfers between devices with their start and end apart: 3 -> 1, of which waited for: 2 -> 0; matrix products, arithmetic and copies ran while one was open for 1% -> 1% of each run, Pallas kernels for 0% -> 0%
where the time goes in v2:
time: 114 us
  blocking collectives  94.4 us (83%)
  Pallas kernels  10.5 us (9%)
  starting transfers between devices  6.49 us (6%)
  local copies, waits for them, and re-layouts  1.77 us (2%)
    all_to_all x2, blocking collectives, spread(): return lax.all_to_all(blocks, axes, 0, 0)  69.6 us
    all_gather x1, blocking collectives, on_device(): weight_rows = lax.all_gather(near[:, 1, :width], 'a', axis=0, tiled=True)  12.6 us
    all_gather x1, blocking collectives, on_device(): upper_rows = lax.all_gather(near[:, 0, :], 'a', axis=0, tiled=True)  12.2 us
    all_to_all x1, starting transfers between devices, spread(): return lax.all_to_all(blocks, axes, 0, 0)  6.49 us
    pallas_call x1, Pallas kernels, third_call(): pl.pallas_call(functools.partial(third_kernel, scale), out_shape=(jax.Sha...  6.44 us
    pallas_call x1, Pallas kernels, second_call(): pl.pallas_call(second_kernel, out_shape=jax.ShapeDtypeStruct((peers, rows...  2.37 us
  transfers between devices with their start and end apart: 1, of which 0 were waited for; matrix products, arithmetic and copies ran while one was open for 1% of the time, Pallas kernels for 0%

profile of v2, /device:TPU:1, one launch (start us, length us, event | category | flops | bytes accessed | tf_op | source)
XLA Modules:
  0.0 113.8 jit_solution(13377866502216867808)
XLA Ops:
  0.6 1.7 %first.1 = bf16[8,2,3456]{2,1,0:T(2,128)(2,1)} custom-call(f32[1,3328]{1,0:T(1,128)} %momentum.3, f32[1,3328]{1,0:T(1,128)} %gradient.3, f32[8,3328]{1,0:T(8,128)} %basis.1, bf16[1,3328]{1,0:T(2,128)(2,1)} %weight.1), custom_call_target="tpu_custom_call" | custom-call | tf_op jit(solution)/shard_map/first/pallas_call | solution.py:130
  2.3 52.4 %all_to_all.15 = bf16[8,2,3456]{2,1,0:T(2,128)(2,1)S(1)} all-to-all(bf16[8,2,3456]{2,1,0:T(2,128)(2,1)} %first.1), channel_id=1, replica_groups=mesh['zh'=8,'zl'=4,'a'=4,'tp'=8] {'zh'}, dimensions={0} | all-to-all | bytes 221184 | tf_op jit(solution)/shard_map/all_to_all | solution.py:22
  54.8 17.2 %all_to_all.16 = bf16[4,8,2,3456]{3,1,2,0:T(8,128)(2,1)S(1)} all-to-all(bf16[4,8,2,3456]{3,1,2,0:T(8,128)(2,1)S(1)} %broadcast_in_dim.2), channel_id=1, replica_groups=mesh['zh'=8,'zl'=4,'a'=4,'tp'=8] {'zl'}, dimensions={0} | all-to-all | bytes 884736 | tf_op jit(solution)/shard_map/all_to_all | solution.py:22
  72.0 12.2 %all-gather = bf16[128,1,3456]{2,0,1:T(8,128)(2,1)} all-gather(bf16[32,1,3456]{2,0,1:T(8,128)(2,1)S(1)} %slice.8), channel_id=2, replica_groups=mesh['zh'=8,'zl'=4,'a'=4,'tp'=8] {'a'}, dimensions={0}, use_global_device_ids=true | all-gather | bytes 1105920 | tf_op jit(solution)/shard_map/all_gather | solution.py:175
  84.2 2.4 %second.1 = f32[8,136,128]{2,1,0:T(8,128)} custom-call(bf16[128,3456]{1,0:T(8,128)(2,1)} %bitcast.10), custom_call_target="tpu_custom_call" | custom-call | tf_op jit(solution)/shard_map/second/pallas_call | solution.py:141
  86.6 0.0 copy-start.1
  86.6 6.5 %all-to-all-start.2 = ((f32[8,136,128]{2,1,0:T(8,128)}), f32[8,136,128]{2,1,0:T(8,128)S(1)}, u32[]{:S(2)}, u32[]{:S(2)}) async-start(f32[8,136,128]{2,1,0:T(8,128)} %second.1), calls=%async_computation.2 | async-start | bytes 1114112 | tf_op jit(solution)/shard_map/all_to_all | solution.py:22
  93.1 0.0 copy-done.1
  93.1 0.1 copy.17
  93.2 0.7 copy.19.inputs
  93.9 12.6 %all-gather.1 = bf16[128,1,3328]{2,0,1:T(8,128)(2,1)} all-gather(bf16[32,1,3328]{2,0,1:T(8,128)(2,1)S(1)} %slice.9), channel_id=3, replica_groups=mesh['zh'=8,'zl'=4,'a'=4,'tp'=8] {'a'}, dimensions={0}, use_global_device_ids=true | all-gather | bytes 1064960 | tf_op jit(solution)/shard_map/all_gather | solution.py:176
  106.6 0.0 all-to-all-done.2.sums
  106.6 0.0 copy-start
  106.6 0.8 copy-done
  107.4 6.4 %third.1 = (f32[1,3328]{1,0:T(1,128)}, f32[8,3328]{1,0:T(8,128)}, bf16[1,3328]{1,0:T(2,128)(2,1)}, bf16[128,3328]{1,0:T(8,128)(2,1)}) custom-call(s32[1]{0:T(128)} %bitcast.place, f32[8,136,128]{2,1,0:T(8,128)} %copy-done, bf16[128,3456]{1,0:T(8,128)(2,1)} %bitcast.11, bf16[128,3328]{1,0:T(8,128)(2,1)} %bitcast.12, f32[1,3328]{1,0:T(1,128)} %momentum.3, ...), custom_call_target="tpu_custom_call" | custom-call | tf_op jit(solution)/shard_map/third/pallas_call | solution.py:152
  (6 shorter events, 0.1 us)
Async XLA Ops:
  86.6 6.5 %copy-start.1 = (bf16[128,128]{1,0:T(8,128)(2,1)S(1)}, bf16[128,128]{1,0:T(8,128)(2,1)}, u32[]{:S(2)}) copy-start(bf16[128,128]{1,0:T(8,128)(2,1)} %param.9) | copy-start | bytes 98308
  86.6 20.0 %all-to-all-start.2 = ((f32[8,136,128]{2,1,0:T(8,128)}), f32[8,136,128]{2,1,0:T(8,128)S(1)}, u32[]{:S(2)}, u32[]{:S(2)}) async-start(f32[8,136,128]{2,1,0:T(8,128)} %second.1), calls=%async_computation.2 | async-start | bytes 1114112 | tf_op jit(solution)/shard_map/all_to_all | solution.py:22
  106.6 0.8 copy-start

commit v3 on v2

--- a/solution.py
+++ b/solution.py
@@ -36,7 +36,18 @@
     return high, middle, x - high - middle
 
 
-def first_kernel(momentum, gradient, basis, weight, out):
+def inverse_root(x):
+    guess = lax.rsqrt(x)
+    return guess * (1.5 - 0.5 * x * guess * guess)
+
+
+def first_kernel(momentum_hbm, gradient_hbm, basis_hbm, weight_hbm, out, momentum, gradient, basis, weight, arrived):
+    pairs = ((momentum_hbm, momentum), (gradient_hbm, gradient), (basis_hbm, basis), (weight_hbm, weight))
+    copies = [pltpu.make_async_copy(source, target, arrived.at[n]) for n, (source, target) in enumerate(pairs)]
+    for copy in copies:
+        copy.start()
+    for copy in copies:
+        copy.wait()
     width = momentum.shape[1]
     rank = basis.shape[0]
     total = jnp.zeros((rank, 128), f32)
@@ -83,29 +94,30 @@
     square, power = total[:rows], total[rows:]
     gram = lax.dot_general(power, power, (((1,), (1,)), ((), ())), precision=highest, preferred_element_type=f32)
     sub = iota((rank, rows), 0)
-    left = jnp.concatenate([gram, jnp.zeros((rank, rows - rank), f32)], axis=1)
+    columns = [jnp.broadcast_to(gram[:, k : k + 1], (rank, rows)) for k in range(rank)]
     ortho = power
     for k in range(rank):
-        column = jnp.broadcast_to(left[:, k : k + 1], (rank, rows))
-        pivot = jnp.broadcast_to(column[k : k + 1], (rank, rows))
-        root = 1.0 / jnp.sqrt(pivot)
-        left_row = left[k : k + 1] * root
-        ortho_row = ortho[k : k + 1] * root
-        factor = column * root
-        left = jnp.where(sub > k, left - factor * left_row, left)
-        ortho = jnp.where(sub > k, ortho - factor * ortho_row, jnp.where(sub == k, ortho_row, ortho))
+        root = inverse_root(jnp.broadcast_to(columns[k][k : k + 1], (rank, rows)))
+        factor = jnp.where(sub > k, columns[k] * root, 0.0)
+        for j in range(k + 1, rank):
+            columns[j] = columns[j] - factor * (columns[j][k : k + 1] * root[:1])
+        ortho_row = ortho[k : k + 1] * root[:1]
+        ortho = jnp.where(sub == k, ortho_row, ortho - factor * ortho_row)
     along = lax.dot_general(ortho, square, (((1,), (0,)), ((), ())), precision=highest, preferred_element_type=f32)
     squares = jnp.maximum(jnp.sum(along * ortho, axis=1, keepdims=True), 0.0)
-    inverse = 1.0 / jnp.sqrt(squares + epsilon)
-    high, middle, low = three_parts(ortho)
-    stacked = jnp.concatenate([high, middle, low], axis=0).astype(bf16)
+    inverse = inverse_root(jnp.broadcast_to(squares, (rank, rows)) + epsilon)[:, :1]
+    stacked = jnp.concatenate(three_parts(ortho), axis=0).astype(bf16)
+    high, middle, low = three_parts(-scale * ortho)
     right_side = jnp.concatenate([high, high, middle, middle, high, low], axis=0)
     turned = jnp.concatenate([right_side, jnp.zeros((rows - 6 * rank, rows), f32)], axis=0).T.astype(bf16)
+    identity = (iota((rows, rows), 0) == iota((rows, rows), 1)).astype(f32).astype(bf16)
+    turned = jnp.concatenate([identity, turned], axis=1)
     here = place[0]
     own = jnp.sum(jnp.where(iota((rank, rows), 1) == here, ortho, 0.0), axis=1, keepdims=True) * (1.0 - decay_rate)
     chosen = (iota((16, rows), 1) == here).astype(f32).astype(bf16)
     left_side = jnp.concatenate([inputs[...], chosen], axis=0)
-    chunk = 256
+    chunk = 1664
+    padding = jnp.zeros((rows - 6 * rank, chunk), f32)
     for start in range(0, width, chunk):
         cut = slice(start, start + chunk)
         parts = jnp.dot(stacked, upper_rows[:, cut], preferred_element_type=f32)
@@ -115,25 +127,29 @@
         basis = coeff * inverse
         new_basis[:, cut] = basis
         high, middle, low = three_parts(basis)
-        under = jnp.concatenate([high, middle, high, middle, low, high], axis=0).astype(bf16)
-        step = jnp.dot(turned[:, : 6 * rank], under, preferred_element_type=f32)
-        fresh = (weight_rows[:, cut].astype(f32) - scale * step).astype(bf16)
+        under = jnp.concatenate([high, middle, high, middle, low, high, padding], axis=0).astype(bf16)
+        mixed = jnp.concatenate([weight_rows[:, cut], under], axis=0)
+        fresh = jnp.dot(turned, mixed, preferred_element_type=f32).astype(bf16)
         result = jnp.dot(left_side, fresh, preferred_element_type=f32).astype(bf16)
         activations[:, cut] = result[: inputs.shape[0]]
         new_weight[:, cut] = result[inputs.shape[0] : inputs.shape[0] + 1]
 
 
 vmem = pl.BlockSpec(memory_space=pltpu.VMEM)
+small_grant = pltpu.CompilerParams(vmem_limit_bytes=16 * 2**20)
 
 
 def first_call(peers, momentum, gradient, basis, weight):
+    arrays = [pltpu.with_memory_space_constraint(x, pltpu.HBM) for x in (momentum, gradient, basis, weight)]
     return pl.pallas_call(
         first_kernel,
         out_shape=jax.ShapeDtypeStruct((peers, 2, momentum.shape[1] + tail), bf16),
-        in_specs=[vmem] * 4,
+        in_specs=[pl.BlockSpec(memory_space=pltpu.HBM)] * 4,
         out_specs=vmem,
+        scratch_shapes=[pltpu.VMEM(x.shape, x.dtype) for x in arrays] + [pltpu.SemaphoreType.DMA((4,))],
+        compiler_params=small_grant,
         name="first",
-    )(momentum, gradient, basis, weight)
+    )(*arrays)
 
 
 def second_call(peers, rank, upper_rows):
@@ -143,6 +159,7 @@
         out_shape=jax.ShapeDtypeStruct((peers, rows + rank, rows), f32),
         in_specs=[vmem],
         out_specs=vmem,
+        compiler_params=small_grant,
         name="second",
     )(upper_rows)
 
@@ -159,6 +176,7 @@
         ),
         in_specs=[pl.BlockSpec(memory_space=pltpu.SMEM)] + [vmem] * 6,
         out_specs=(vmem,) * 4,
+        compiler_params=small_grant,
         name="third",
     )(place, sums, upper_rows, weight_rows, momentum, gradient, inputs)
 

time: 114 us -> 107 us (0.939)
  Pallas kernels: 10.5 us -> 4.72 us
  local copies, waits for them, and re-layouts: 1.77 us -> 0.36 us
    pallas_call x1, Pallas kernels: 6.44 us -> 2.41 us  [third_call(): pl.pallas_call(functools.partial(third_kernel, scale), out_shape=(jax.Sha...]
    pallas_call x1, Pallas kernels: 2.37 us -> 1.22 us  [second_call(): pl.pallas_call(second_kernel, out_shape=jax.ShapeDtypeStruct((peers, rows...]
  transfers between devices with their start and end apart: 1 -> 1, of which waited for: 0 -> 0; matrix products, arithmetic and copies ran while one was open for 1% -> 0% of each run, Pallas kernels for 0% -> 0%
where the time goes in v3:
time: 107 us; the launch traced here: 106 us
  blocking collectives  93.8 us (88%)
  starting transfers between devices  6.48 us (6%)
  Pallas kernels  4.72 us (4%)
    all_to_all x2, blocking collectives, spread(): return lax.all_to_all(blocks, axes, 0, 0)  69.4 us
    all_gather x1, blocking collectives, on_device(): weight_rows = lax.all_gather(near[:, 1, :width], 'a', axis=0, tiled=True)  12.7 us
    all_gather x1, blocking collectives, on_device(): upper_rows = lax.all_gather(near[:, 0, :], 'a', axis=0, tiled=True)  11.7 us
    all_to_all x1, starting transfers between devices, spread(): return lax.all_to_all(blocks, axes, 0, 0)  6.48 us
    pallas_call x1, Pallas kernels, third_call(): pl.pallas_call(functools.partial(third_kernel, scale), out_shape=(jax.Sha...  2.41 us
  transfers between devices with their start and end apart: 1, of which 0 were waited for; matrix products, arithmetic and copies ran while one was open for 0% of the time, Pallas kernels for 0%

profile of v3, /device:TPU:1, one launch (start us, length us, event | category | flops | bytes accessed | tf_op | source)
XLA Modules:
  0.0 106.1 jit_solution(6162484863305102572)
XLA Ops:
  0.6 1.1 %first.1 = bf16[8,2,3456]{2,1,0:T(2,128)(2,1)S(1)} custom-call(f32[1,3328]{1,0:T(1,128)} %momentum.1, f32[1,3328]{1,0:T(1,128)} %gradient.1, f32[8,3328]{1,0:T(8,128)} %basis_hbm.1, bf16[1,3328]{1,0:T(2,128)(2,1)} %weight_hbm.1), custom_call_target="tpu_custom_call" | custom-call | tf_op jit(solution)/shard_map/first/pallas_call | solution.py:144
  1.7 52.2 %all_to_all.15 = bf16[8,2,3456]{2,1,0:T(2,128)(2,1)S(1)} all-to-all(bf16[8,2,3456]{2,1,0:T(2,128)(2,1)S(1)} %first.1), channel_id=1, replica_groups=mesh['zh'=8,'zl'=4,'a'=4,'tp'=8] {'zh'}, dimensions={0} | all-to-all | bytes 221184 | tf_op jit(solution)/shard_map/all_to_all | solution.py:22
  54.0 17.2 %all_to_all.16 = bf16[4,8,2,3456]{3,1,2,0:T(8,128)(2,1)S(1)} all-to-all(bf16[4,8,2,3456]{3,1,2,0:T(8,128)(2,1)S(1)} %broadcast_in_dim.2), channel_id=1, replica_groups=mesh['zh'=8,'zl'=4,'a'=4,'tp'=8] {'zl'}, dimensions={0} | all-to-all | bytes 884736 | tf_op jit(solution)/shard_map/all_to_all | solution.py:22
  71.2 11.7 %all-gather = bf16[128,1,3456]{2,0,1:T(8,128)(2,1)S(1)} all-gather(bf16[32,1,3456]{2,0,1:T(8,128)(2,1)S(1)} %slice.8), channel_id=2, replica_groups=mesh['zh'=8,'zl'=4,'a'=4,'tp'=8] {'a'}, dimensions={0}, use_global_device_ids=true | all-gather | bytes 1105920 | tf_op jit(solution)/shard_map/all_gather | solution.py:193
  82.9 1.2 %second.1 = f32[8,136,128]{2,1,0:T(8,128)} custom-call(bf16[128,3456]{1,0:T(8,128)(2,1)S(1)} %bitcast.10), custom_call_target="tpu_custom_call" | custom-call | tf_op jit(solution)/shard_map/second/pallas_call | solution.py:157
  84.2 0.0 copy-start.2
  84.2 6.5 %all-to-all-start.2 = ((f32[8,136,128]{2,1,0:T(8,128)}), f32[8,136,128]{2,1,0:T(8,128)S(1)}, u32[]{:S(2)}, u32[]{:S(2)}) async-start(f32[8,136,128]{2,1,0:T(8,128)} %second.1), calls=%async_computation.2 | async-start | bytes 1114112 | tf_op jit(solution)/shard_map/all_to_all | solution.py:22
  90.6 0.0 copy-done.2
  90.7 0.1 copy.17
  90.8 0.1 copy.19.inputs
  90.9 0.0 copy-start
  91.0 0.0 copy-start.1
  91.0 12.7 %all-gather.1 = bf16[128,1,3328]{2,0,1:T(8,128)(2,1)S(1)} all-gather(bf16[32,1,3328]{2,0,1:T(8,128)(2,1)S(1)} %slice.9), channel_id=3, replica_groups=mesh['zh'=8,'zl'=4,'a'=4,'tp'=8] {'a'}, dimensions={0}, use_global_device_ids=true | all-gather | bytes 1064960 | tf_op jit(solution)/shard_map/all_gather | solution.py:194
  103.7 0.0 all-to-all-done.2.sums
  103.7 0.0 copy-done
  103.7 0.0 copy-done.1
  103.7 2.4 %third.1 = (f32[1,3328]{1,0:T(1,128)}, f32[8,3328]{1,0:T(8,128)}, bf16[1,3328]{1,0:T(2,128)(2,1)}, bf16[128,3328]{1,0:T(8,128)(2,1)}) custom-call(s32[1]{0:T(128)} %bitcast.place, f32[8,136,128]{2,1,0:T(8,128)S(1)} %all-to-all-done.2.sums, bf16[128,3456]{1,0:T(8,128)(2,1)S(1)} %bitcast.11, bf16[128,3328]{1,0:T(8,128)(2,1)S(1)} %bitcast.12, ...), custom_call_target="tpu_custom_call" | custom-call | tf_op jit(solution)/shard_map/third/pallas_call | solution.py:169
  (6 shorter events, 0.1 us)
Async XLA Ops:
  84.2 6.5 %copy-start.2 = (bf16[128,128]{1,0:T(8,128)(2,1)S(1)}, bf16[128,128]{1,0:T(8,128)(2,1)}, u32[]{:S(2)}) copy-start(bf16[128,128]{1,0:T(8,128)(2,1)} %param.9) | copy-start | bytes 98308
  84.2 19.5 %all-to-all-start.2 = ((f32[8,136,128]{2,1,0:T(8,128)}), f32[8,136,128]{2,1,0:T(8,128)S(1)}, u32[]{:S(2)}, u32[]{:S(2)}) async-start(f32[8,136,128]{2,1,0:T(8,128)} %second.1), calls=%async_computation.2 | async-start | bytes 1114112 | tf_op jit(solution)/shard_map/all_to_all | solution.py:22
  90.9 12.8 %copy-start = (f32[1,3328]{1,0:T(1,128)S(1)}, f32[1,3328]{1,0:T(1,128)}, u32[]{:S(2)}) copy-start(f32[1,3328]{1,0:T(1,128)} %momentum.1) | copy-start | bytes 39940
  91.0 12.7 %copy-start.1 = (f32[1,3328]{1,0:T(1,128)S(1)}, f32[1,3328]{1,0:T(1,128)}, u32[]{:S(2)}) copy-start(f32[1,3328]{1,0:T(1,128)} %gradient.1) | copy-start | bytes 39940

commit v4 on v3

--- a/solution.py
+++ b/solution.py
@@ -12,7 +12,7 @@
 step_size = 0.5
 epsilon = 1e-06
 highest = lax.Precision.HIGHEST
-rows_axes = ("zh", "zl", "a")
+rows_axes = ("zh", "zl", "xl", "c")
 tail = 128
 bf16 = jnp.bfloat16
 f32 = jnp.float32
@@ -73,14 +73,35 @@
 def second_kernel(upper_rows, out):
     rows = upper_rows.shape[0]
     width = upper_rows.shape[1] - tail
-    rank = out.shape[1] - rows
+    half, quarter = rows // 2, rows // 4
+    rank = out.shape[1] - half - quarter
     buffer = upper_rows[:, :width]
     square = lax.dot_general(buffer, buffer, (((1,), (1,)), ((), ())), preferred_element_type=f32)
+    corner = pltpu.roll(square[half + quarter :], quarter, 1)
+    folded = jnp.where(iota((quarter, rows), 1) < quarter, corner, square[half : half + quarter])
     coded = upper_rows[:, width:].astype(f32).T
     power = coded[:rank] + coded[rank : 2 * rank] + coded[2 * rank : 3 * rank]
     for peer in range(out.shape[0]):
-        out[peer, :rows] = square
-        out[peer, rows:] = power
+        out[peer, :half] = square[:half]
+        out[peer, half : half + quarter] = folded
+        out[peer, half + quarter :] = power
+
+
+def quadratic(folded, vectors):
+    rank, rows = vectors.shape
+    half, quarter = rows // 2, rows // 4
+    lane = iota((rank, rows), 1)
+    in_third = (lane >= half) & (lane < half + quarter)
+    turned = pltpu.roll(vectors, rows - quarter, 1)
+    left = jnp.concatenate(
+        [jnp.where(lane < half, vectors, 0.0), jnp.where(in_third, vectors, 0.0), jnp.where(in_third, turned, 0.0)], axis=0
+    )
+    right = jnp.concatenate([folded, jnp.zeros((quarter, rows), f32)], axis=0)
+    along = lax.dot_general(left, right, (((1,), (0,)), ((), ())), precision=highest, preferred_element_type=f32)
+    top = along[:rank] * vectors * jnp.where(lane < half, 1.0, 2.0)
+    middle = along[rank : 2 * rank] * vectors * jnp.where(lane < half, 0.0, jnp.where(lane < half + quarter, 1.0, 2.0))
+    corner = jnp.where(lane < quarter, along[2 * rank :] * pltpu.roll(vectors, quarter, 1), 0.0)
+    return jnp.sum(top + middle + corner, axis=1, keepdims=True)
 
 
 def third_kernel(
@@ -91,7 +112,7 @@
     total = sums[0]
     for peer in range(1, sums.shape[0]):
         total = total + sums[peer]
-    square, power = total[:rows], total[rows:]
+    folded, power = total[:-rank], total[-rank:]
     gram = lax.dot_general(power, power, (((1,), (1,)), ((), ())), precision=highest, preferred_element_type=f32)
     sub = iota((rank, rows), 0)
     columns = [jnp.broadcast_to(gram[:, k : k + 1], (rank, rows)) for k in range(rank)]
@@ -103,36 +124,29 @@
             columns[j] = columns[j] - factor * (columns[j][k : k + 1] * root[:1])
         ortho_row = ortho[k : k + 1] * root[:1]
         ortho = jnp.where(sub == k, ortho_row, ortho - factor * ortho_row)
-    along = lax.dot_general(ortho, square, (((1,), (0,)), ((), ())), precision=highest, preferred_element_type=f32)
-    squares = jnp.maximum(jnp.sum(along * ortho, axis=1, keepdims=True), 0.0)
+    squares = jnp.maximum(quadratic(folded, ortho), 0.0)
     inverse = inverse_root(jnp.broadcast_to(squares, (rank, rows)) + epsilon)[:, :1]
     stacked = jnp.concatenate(three_parts(ortho), axis=0).astype(bf16)
     high, middle, low = three_parts(-scale * ortho)
     right_side = jnp.concatenate([high, high, middle, middle, high, low], axis=0)
     turned = jnp.concatenate([right_side, jnp.zeros((rows - 6 * rank, rows), f32)], axis=0).T.astype(bf16)
-    identity = (iota((rows, rows), 0) == iota((rows, rows), 1)).astype(f32).astype(bf16)
-    turned = jnp.concatenate([identity, turned], axis=1)
     here = place[0]
     own = jnp.sum(jnp.where(iota((rank, rows), 1) == here, ortho, 0.0), axis=1, keepdims=True) * (1.0 - decay_rate)
     chosen = (iota((16, rows), 1) == here).astype(f32).astype(bf16)
     left_side = jnp.concatenate([inputs[...], chosen], axis=0)
-    chunk = 1664
-    padding = jnp.zeros((rows - 6 * rank, chunk), f32)
-    for start in range(0, width, chunk):
-        cut = slice(start, start + chunk)
-        parts = jnp.dot(stacked, upper_rows[:, cut], preferred_element_type=f32)
-        coeff = parts[:rank] + parts[rank : 2 * rank] + parts[2 * rank :]
-        buffer = decay_rate * momentum[:, cut] + gradient[:, cut]
-        new_momentum[:, cut] = buffer - jnp.sum(own * coeff, axis=0, keepdims=True)
-        basis = coeff * inverse
-        new_basis[:, cut] = basis
-        high, middle, low = three_parts(basis)
-        under = jnp.concatenate([high, middle, high, middle, low, high, padding], axis=0).astype(bf16)
-        mixed = jnp.concatenate([weight_rows[:, cut], under], axis=0)
-        fresh = jnp.dot(turned, mixed, preferred_element_type=f32).astype(bf16)
-        result = jnp.dot(left_side, fresh, preferred_element_type=f32).astype(bf16)
-        activations[:, cut] = result[: inputs.shape[0]]
-        new_weight[:, cut] = result[inputs.shape[0] : inputs.shape[0] + 1]
+    parts = jnp.dot(stacked, upper_rows[:, :width], preferred_element_type=f32)
+    coeff = parts[:rank] + parts[rank : 2 * rank] + parts[2 * rank :]
+    buffer = decay_rate * momentum[...] + gradient[...]
+    new_momentum[...] = buffer - jnp.sum(own * coeff, axis=0, keepdims=True)
+    basis = coeff * inverse
+    new_basis[...] = basis
+    high, middle, low = three_parts(basis)
+    under = jnp.concatenate([high, middle, high, middle, low, high], axis=0).astype(bf16)
+    step = jnp.dot(turned[:, : 6 * rank], under, preferred_element_type=f32)
+    fresh = (weight_rows[...].astype(f32) + step).astype(bf16)
+    result = jnp.dot(left_side, fresh, preferred_element_type=f32).astype(bf16)
+    activations[...] = result[: inputs.shape[0]]
+    new_weight[...] = result[inputs.shape[0] : inputs.shape[0] + 1]
 
 
 vmem = pl.BlockSpec(memory_space=pltpu.VMEM)
@@ -156,7 +170,7 @@
     rows = upper_rows.shape[0]
     return pl.pallas_call(
         second_kernel,
-        out_shape=jax.ShapeDtypeStruct((peers, rows + rank, rows), f32),
+        out_shape=jax.ShapeDtypeStruct((peers, rows // 2 + rows // 4 + rank, rows), f32),
         in_specs=[vmem],
         out_specs=vmem,
         compiler_params=small_grant,
@@ -182,19 +196,19 @@
 
 
 def on_device(momentum, gradient, basis, weight, inputs):
-    zh, zl, a = (lax.axis_size(n) for n in rows_axes)
-    rows = zh * zl * a
+    zh, zl, xl, c = (lax.axis_size(n) for n in rows_axes)
+    rows = zh * zl * xl * c
     width = momentum.shape[1]
     rank = basis.shape[0]
     peers = lax.axis_size("tp")
     scale = step_size * math.sqrt(width * peers / rows)
     far = spread(first_call(zh, momentum, gradient, basis, weight), "zh")
-    near = spread(replicated(far, "zl"), "zl").reshape(zl * zh, 2, width + tail)
-    upper_rows = lax.all_gather(near[:, 0, :], "a", axis=0, tiled=True)
-    weight_rows = lax.all_gather(near[:, 1, :width], "a", axis=0, tiled=True)
+    near = spread(replicated(far, ("zl", "xl")), ("zl", "xl")).reshape(zl * xl * zh, 2, width + tail)
+    upper_rows = lax.all_gather(near[:, 0, :], "c", axis=0, tiled=True)
+    weight_rows = lax.all_gather(near[:, 1, :width], "c", axis=0, tiled=True)
     sums = spread(second_call(peers, rank, upper_rows), "tp")
-    place = (lax.axis_index("a") * zl + lax.axis_index("zl")) * zh + lax.axis_index("zh")
-    ordered = inputs.reshape(-1, zh, zl, a).transpose(0, 3, 2, 1).reshape(-1, rows)
+    place = ((lax.axis_index("c") * zl + lax.axis_index("zl")) * xl + lax.axis_index("xl")) * zh + lax.axis_index("zh")
+    ordered = inputs.reshape(-1, zh, zl, xl, c).transpose(0, 4, 2, 3, 1).reshape(-1, rows)
     return third_call(
         scale, rank, place.reshape(1).astype(jnp.int32), sums, upper_rows, weight_rows, momentum, gradient, ordered
     )
@@ -202,7 +216,7 @@
 
 def solution(mesh):
     fsdp, tp = mesh.devices.shape
-    fine = Mesh(mesh.devices.reshape(fsdp // 16, 4, 4, tp), rows_axes + ("tp",))
+    fine = Mesh(mesh.devices.reshape(fsdp // 16, 4, 2, 2, tp), rows_axes + ("tp",))
     return jax.shard_map(
         on_device,
         mesh=fine,

time: 107 us -> 107 us (level)
  waiting for transfers between devices: 0.01 us -> 6.94 us
  blocking collectives: 93.8 us -> 87.8 us
    all_gather x2, blocking collectives: 24.4 us -> 7.45 us  [the longest x1 4.76 us: on_device(): upper_rows = lax.all_gather(near[:, 0, :], 'c', axis=0, tiled=True)]
    all_to_all x2, blocking collectives: 69.4 us -> 80.4 us  [spread(): return lax.all_to_all(blocks, axes, 0, 0)]
    all_to_all x1, waiting for transfers between devices: 0.01 us -> 6.94 us  [spread(): return lax.all_to_all(blocks, axes, 0, 0)]
  transfers between devices with their start and end apart: 1 -> 1, of which waited for: 0 -> 1; matrix products, arithmetic and copies ran while one was open for 0% -> 0% of each run, Pallas kernels for 0% -> 0%
where the time goes in v4:
time: 107 us
  blocking collectives  87.8 us (82%)
  waiting for transfers between devices  6.94 us (6%)
  starting transfers between devices  6.5 us (6%)
  Pallas kernels  4.5 us (4%)
    all_to_all x2, blocking collectives, spread(): return lax.all_to_all(blocks, axes, 0, 0)  80.4 us
    all_to_all x1, waiting for transfers between devices, spread(): return lax.all_to_all(blocks, axes, 0, 0)  6.94 us
    all_to_all x1, starting transfers between devices, spread(): return lax.all_to_all(blocks, axes, 0, 0)  6.5 us
    all_gather x1, blocking collectives, on_device(): upper_rows = lax.all_gather(near[:, 0, :], 'c', axis=0, tiled=True)  4.76 us
    all_gather x1, blocking collectives, on_device(): weight_rows = lax.all_gather(near[:, 1, :width], 'c', axis=0, tiled=True)  2.69 us
    pallas_call x1, Pallas kernels, third_call(): pl.pallas_call(functools.partial(third_kernel, scale), out_shape=(jax.Sha...  2.19 us
  transfers between devices with their start and end apart: 1, of which 1 were waited for; matrix products, arithmetic and copies ran while one was open for 0% of the time, Pallas kernels for 0%

profile of v4, /device:TPU:1, one launch (start us, length us, event | category | flops | bytes accessed | tf_op | source)
XLA Modules:
  0.0 107.0 jit_solution(15163047416650128987)
XLA Ops:
  0.6 1.1 %first.1 = bf16[8,2,3456]{2,1,0:T(2,128)(2,1)S(1)} custom-call(f32[1,3328]{1,0:T(1,128)} %momentum.1, f32[1,3328]{1,0:T(1,128)} %gradient.1, f32[8,3328]{1,0:T(8,128)} %basis_hbm.1, bf16[1,3328]{1,0:T(2,128)(2,1)} %weight_hbm.1), custom_call_target="tpu_custom_call" | custom-call | tf_op jit(solution)/shard_map/first/pallas_call | solution.py:158
  1.7 52.2 %all_to_all.15 = bf16[8,2,3456]{2,1,0:T(2,128)(2,1)S(1)} all-to-all(bf16[8,2,3456]{2,1,0:T(2,128)(2,1)S(1)} %first.1), channel_id=1, replica_groups=mesh['zh'=8,'zl'=4,'xl'=2,'c'=2,'tp'=8] {'zh'}, dimensions={0} | all-to-all | bytes 221184 | tf_op jit(solution)/shard_map/all_to_all | solution.py:22
  54.0 0.1 broadcast_in_dim.2
  54.0 28.2 %all_to_all.16 = bf16[8,8,2,3456]{3,1,2,0:T(8,128)(2,1)S(1)} all-to-all(bf16[8,8,2,3456]{3,1,2,0:T(8,128)(2,1)S(1)} %broadcast_in_dim.2), channel_id=1, replica_groups=mesh['zh'=8,'zl'=4,'xl'=2,'c'=2,'tp'=8] {'zl','xl'}, dimensions={0} | all-to-all | bytes 1769472 | tf_op jit(solution)/shard_map/all_to_all | solution.py:22
  82.2 0.1 copy.21
  82.3 4.8 %all-gather = bf16[128,1,3456]{2,0,1:T(8,128)(2,1)S(1)} all-gather(bf16[64,1,3456]{2,0,1:T(8,128)(2,1)S(1)} %slice.8), channel_id=2, replica_groups=mesh['zh'=8,'zl'=4,'xl'=2,'c'=2,'tp'=8] {'c'}, dimensions={0}, use_global_device_ids=true | all-gather | bytes 1327104 | tf_op jit(solution)/shard_map/all_gather | solution.py:207
  87.1 1.2 %second.1 = f32[8,104,128]{2,1,0:T(8,128)} custom-call(bf16[128,3456]{1,0:T(8,128)(2,1)S(1)} %bitcast.10), custom_call_target="tpu_custom_call" | custom-call | tf_op jit(solution)/shard_map/second/pallas_call | solution.py:171
  88.3 0.0 copy-start.2
  88.3 6.5 %all-to-all-start.2 = ((f32[8,104,128]{2,1,0:T(8,128)}), f32[8,104,128]{2,1,0:T(8,128)S(1)}, u32[]{:S(2)}, u32[]{:S(2)}) async-start(f32[8,104,128]{2,1,0:T(8,128)} %second.1), calls=%async_computation.2 | async-start | bytes 851968 | tf_op jit(solution)/shard_map/all_to_all | solution.py:22
  94.8 0.0 copy-done.2
  94.8 0.1 copy.17
  94.9 0.1 copy.19.inputs
  95.1 0.0 copy-start
  95.1 0.0 copy-start.1
  95.1 2.7 %all-gather.1 = bf16[128,1,3328]{2,0,1:T(8,128)(2,1)S(1)} all-gather(bf16[64,1,3328]{2,0,1:T(8,128)(2,1)S(1)} %slice.9), channel_id=3, replica_groups=mesh['zh'=8,'zl'=4,'xl'=2,'c'=2,'tp'=8] {'c'}, dimensions={0}, use_global_device_ids=true | all-gather | bytes 1277952 | tf_op jit(solution)/shard_map/all_gather | solution.py:208
  97.8 6.9 %all-to-all-done.2.sums = f32[8,104,128]{2,1,0:T(8,128)S(1)} async-done(((f32[8,104,128]{2,1,0:T(8,128)}), f32[8,104,128]{2,1,0:T(8,128)S(1)}, u32[]{:S(2)}, u32[]{:S(2)}) %all-to-all-start.2) | async-done | bytes 426016 | tf_op jit(solution)/shard_map/all_to_all | solution.py:22
  104.8 0.0 copy-done
  104.8 0.0 copy-done.1
  104.8 2.2 %third.1 = (f32[1,3328]{1,0:T(1,128)}, f32[8,3328]{1,0:T(8,128)}, bf16[1,3328]{1,0:T(2,128)(2,1)}, bf16[128,3328]{1,0:T(8,128)(2,1)}) custom-call(s32[1]{0:T(128)} %bitcast.place, f32[8,104,128]{2,1,0:T(8,128)S(1)} %all-to-all-done.2.sums, bf16[128,3456]{1,0:T(8,128)(2,1)S(1)} %bitcast.11, bf16[128,3328]{1,0:T(8,128)(2,1)S(1)} %bitcast.12, ...), custom_call_target="tpu_custom_call" | custom-call | tf_op jit(solution)/shard_map/third/pallas_call | solution.py:183
  (4 shorter events, 0.1 us)
Async XLA Ops:
  88.3 6.5 %copy-start.2 = (bf16[128,128]{1,0:T(8,128)(2,1)S(1)}, bf16[128,128]{1,0:T(8,128)(2,1)}, u32[]{:S(2)}) copy-start(bf16[128,128]{1,0:T(8,128)(2,1)} %param.9) | copy-start | bytes 98308
  88.3 16.5 %all-to-all-start.2 = ((f32[8,104,128]{2,1,0:T(8,128)}), f32[8,104,128]{2,1,0:T(8,128)S(1)}, u32[]{:S(2)}, u32[]{:S(2)}) async-start(f32[8,104,128]{2,1,0:T(8,128)} %second.1), calls=%async_computation.2 | async-start | bytes 851968 | tf_op jit(solution)/shard_map/all_to_all | solution.py:22
  95.1 9.7 %copy-start = (f32[1,3328]{1,0:T(1,128)S(1)}, f32[1,3328]{1,0:T(1,128)}, u32[]{:S(2)}) copy-start(f32[1,3328]{1,0:T(1,128)} %momentum.1) | copy-start | bytes 39940
  95.1 9.7 %copy-start.1 = (f32[1,3328]{1,0:T(1,128)S(1)}, f32[1,3328]{1,0:T(1,128)}, u32[]{:S(2)}) copy-start(f32[1,3328]{1,0:T(1,128)} %gradient.1) | copy-start | bytes 39940

commit v5 on v4

--- a/solution.py
+++ b/solution.py
@@ -12,7 +12,7 @@
 step_size = 0.5
 epsilon = 1e-06
 highest = lax.Precision.HIGHEST
-rows_axes = ("zh", "zl", "xl", "c")
+rows_axes = ("zh", "zl", "a")
 tail = 128
 bf16 = jnp.bfloat16
 f32 = jnp.float32
@@ -196,19 +196,19 @@
 
 
 def on_device(momentum, gradient, basis, weight, inputs):
-    zh, zl, xl, c = (lax.axis_size(n) for n in rows_axes)
-    rows = zh * zl * xl * c
+    zh, zl, a = (lax.axis_size(n) for n in rows_axes)
+    rows = zh * zl * a
     width = momentum.shape[1]
     rank = basis.shape[0]
     peers = lax.axis_size("tp")
     scale = step_size * math.sqrt(width * peers / rows)
     far = spread(first_call(zh, momentum, gradient, basis, weight), "zh")
-    near = spread(replicated(far, ("zl", "xl")), ("zl", "xl")).reshape(zl * xl * zh, 2, width + tail)
-    upper_rows = lax.all_gather(near[:, 0, :], "c", axis=0, tiled=True)
-    weight_rows = lax.all_gather(near[:, 1, :width], "c", axis=0, tiled=True)
+    near = spread(replicated(far, "zl"), "zl").reshape(zl * zh, 2, width + tail)
+    upper_rows = lax.all_gather(near[:, 0, :], "a", axis=0, tiled=True)
+    weight_rows = lax.all_gather(near[:, 1, :width], "a", axis=0, tiled=True)
     sums = spread(second_call(peers, rank, upper_rows), "tp")
-    place = ((lax.axis_index("c") * zl + lax.axis_index("zl")) * xl + lax.axis_index("xl")) * zh + lax.axis_index("zh")
-    ordered = inputs.reshape(-1, zh, zl, xl, c).transpose(0, 4, 2, 3, 1).reshape(-1, rows)
+    place = (lax.axis_index("a") * zl + lax.axis_index("zl")) * zh + lax.axis_index("zh")
+    ordered = inputs.reshape(-1, zh, zl, a).transpose(0, 3, 2, 1).reshape(-1, rows)
     return third_call(
         scale, rank, place.reshape(1).astype(jnp.int32), sums, upper_rows, weight_rows, momentum, gradient, ordered
     )
@@ -216,7 +216,7 @@
 
 def solution(mesh):
     fsdp, tp = mesh.devices.shape
-    fine = Mesh(mesh.devices.reshape(fsdp // 16, 4, 2, 2, tp), rows_axes + ("tp",))
+    fine = Mesh(mesh.devices.reshape(fsdp // 16, 4, 4, tp), rows_axes + ("tp",))
     return jax.shard_map(
         on_device,
         mesh=fine,

time: 107 us -> 105 us (0.981)
  waiting for transfers between devices: 6.94 us -> 0.01 us
  blocking collectives: 87.8 us -> 92.4 us
    all_gather x2, blocking collectives: 7.45 us -> 23 us  [the longest x1 11.7 us: on_device(): upper_rows = lax.all_gather(near[:, 0, :], 'a', axis=0, tiled=True)]
    all_to_all x2, blocking collectives: 80.4 us -> 69.4 us  [spread(): return lax.all_to_all(blocks, axes, 0, 0)]
    all_to_all x1, waiting for transfers between devices: 6.94 us -> 0.01 us  [spread(): return lax.all_to_all(blocks, axes, 0, 0)]
  transfers between devices with their start and end apart: 1 -> 1, of which waited for: 1 -> 0; matrix products, arithmetic and copies ran while one was open for 0% -> 0% of each run, Pallas kernels for 0% -> 0%
where the time goes in v5:
time: 105 us
  blocking collectives  92.4 us (88%)
  starting transfers between devices  6.48 us (6%)
  Pallas kernels  4.52 us (4%)
    all_to_all x2, blocking collectives, spread(): return lax.all_to_all(blocks, axes, 0, 0)  69.4 us
    all_gather x1, blocking collectives, on_device(): upper_rows = lax.all_gather(near[:, 0, :], 'a', axis=0, tiled=True)  11.7 us
    all_gather x1, blocking collectives, on_device(): weight_rows = lax.all_gather(near[:, 1, :width], 'a', axis=0, tiled=True)  11.3 us
    all_to_all x1, starting transfers between devices, spread(): return lax.all_to_all(blocks, axes, 0, 0)  6.48 us
    pallas_call x1, Pallas kernels, third_call(): pl.pallas_call(functools.partial(third_kernel, scale), out_shape=(jax.Sha...  2.19 us
  transfers between devices with their start and end apart: 1, of which 0 were waited for; matrix products, arithmetic and copies ran while one was open for 0% of the time, Pallas kernels for 0%

profile of v5, /device:TPU:1, one launch (start us, length us, event | category | flops | bytes accessed | tf_op | source)
XLA Modules:
  0.0 104.5 jit_solution(7511069606445078367)
XLA Ops:
  0.6 1.1 %first.1 = bf16[8,2,3456]{2,1,0:T(2,128)(2,1)S(1)} custom-call(f32[1,3328]{1,0:T(1,128)} %momentum.1, f32[1,3328]{1,0:T(1,128)} %gradient.1, f32[8,3328]{1,0:T(8,128)} %basis_hbm.1, bf16[1,3328]{1,0:T(2,128)(2,1)} %weight_hbm.1), custom_call_target="tpu_custom_call" | custom-call | tf_op jit(solution)/shard_map/first/pallas_call | solution.py:158
  1.7 52.2 %all_to_all.15 = bf16[8,2,3456]{2,1,0:T(2,128)(2,1)S(1)} all-to-all(bf16[8,2,3456]{2,1,0:T(2,128)(2,1)S(1)} %first.1), channel_id=1, replica_groups=mesh['zh'=8,'zl'=4,'a'=4,'tp'=8] {'zh'}, dimensions={0} | all-to-all | bytes 221184 | tf_op jit(solution)/shard_map/all_to_all | solution.py:22
  54.0 17.2 %all_to_all.16 = bf16[4,8,2,3456]{3,1,2,0:T(8,128)(2,1)S(1)} all-to-all(bf16[4,8,2,3456]{3,1,2,0:T(8,128)(2,1)S(1)} %broadcast_in_dim.2), channel_id=1, replica_groups=mesh['zh'=8,'zl'=4,'a'=4,'tp'=8] {'zl'}, dimensions={0} | all-to-all | bytes 884736 | tf_op jit(solution)/shard_map/all_to_all | solution.py:22
  71.2 11.7 %all-gather = bf16[128,1,3456]{2,0,1:T(8,128)(2,1)S(1)} all-gather(bf16[32,1,3456]{2,0,1:T(8,128)(2,1)S(1)} %slice.8), channel_id=2, replica_groups=mesh['zh'=8,'zl'=4,'a'=4,'tp'=8] {'a'}, dimensions={0}, use_global_device_ids=true | all-gather | bytes 1105920 | tf_op jit(solution)/shard_map/all_gather | solution.py:207
  82.9 1.2 %second.1 = f32[8,104,128]{2,1,0:T(8,128)} custom-call(bf16[128,3456]{1,0:T(8,128)(2,1)S(1)} %bitcast.10), custom_call_target="tpu_custom_call" | custom-call | tf_op jit(solution)/shard_map/second/pallas_call | solution.py:171
  84.2 0.0 copy-start.2
  84.2 6.5 %all-to-all-start.2 = ((f32[8,104,128]{2,1,0:T(8,128)}), f32[8,104,128]{2,1,0:T(8,128)S(1)}, u32[]{:S(2)}, u32[]{:S(2)}) async-start(f32[8,104,128]{2,1,0:T(8,128)} %second.1), calls=%async_computation.2 | async-start | bytes 851968 | tf_op jit(solution)/shard_map/all_to_all | solution.py:22
  90.7 0.0 copy-done.2
  90.7 0.1 copy.17
  90.8 0.1 copy.19.inputs
  91.0 0.0 copy-start
  91.0 0.0 copy-start.1
  91.0 11.3 %all-gather.1 = bf16[128,1,3328]{2,0,1:T(8,128)(2,1)S(1)} all-gather(bf16[32,1,3328]{2,0,1:T(8,128)(2,1)S(1)} %slice.9), channel_id=3, replica_groups=mesh['zh'=8,'zl'=4,'a'=4,'tp'=8] {'a'}, dimensions={0}, use_global_device_ids=true | all-gather | bytes 1064960 | tf_op jit(solution)/shard_map/all_gather | solution.py:208
  102.3 0.0 all-to-all-done.2.sums
  102.3 0.0 copy-done
  102.3 0.0 copy-done.1
  102.3 2.2 %third.1 = (f32[1,3328]{1,0:T(1,128)}, f32[8,3328]{1,0:T(8,128)}, bf16[1,3328]{1,0:T(2,128)(2,1)}, bf16[128,3328]{1,0:T(8,128)(2,1)}) custom-call(s32[1]{0:T(128)} %bitcast.place, f32[8,104,128]{2,1,0:T(8,128)S(1)} %all-to-all-done.2.sums, bf16[128,3456]{1,0:T(8,128)(2,1)S(1)} %bitcast.11, bf16[128,3328]{1,0:T(8,128)(2,1)S(1)} %bitcast.12, ...), custom_call_target="tpu_custom_call" | custom-call | tf_op jit(solution)/shard_map/third/pallas_call | solution.py:183
  (6 shorter events, 0.1 us)
Async XLA Ops:
  84.2 6.5 %copy-start.2 = (bf16[128,128]{1,0:T(8,128)(2,1)S(1)}, bf16[128,128]{1,0:T(8,128)(2,1)}, u32[]{:S(2)}) copy-start(bf16[128,128]{1,0:T(8,128)(2,1)} %param.9) | copy-start | bytes 98308
  84.2 18.1 %all-to-all-start.2 = ((f32[8,104,128]{2,1,0:T(8,128)}), f32[8,104,128]{2,1,0:T(8,128)S(1)}, u32[]{:S(2)}, u32[]{:S(2)}) async-start(f32[8,104,128]{2,1,0:T(8,128)} %second.1), calls=%async_computation.2 | async-start | bytes 851968 | tf_op jit(solution)/shard_map/all_to_all | solution.py:22
  91.0 11.4 %copy-start = (f32[1,3328]{1,0:T(1,128)S(1)}, f32[1,3328]{1,0:T(1,128)}, u32[]{:S(2)}) copy-start(f32[1,3328]{1,0:T(1,128)} %momentum.1) | copy-start | bytes 39940
  91.0 11.3 %copy-start.1 = (f32[1,3328]{1,0:T(1,128)S(1)}, f32[1,3328]{1,0:T(1,128)}, u32[]{:S(2)}) copy-start(f32[1,3328]{1,0:T(1,128)} %gradient.1) | copy-start | bytes 39940

commit v6 on v4

--- a/solution.py
+++ b/solution.py
@@ -105,7 +105,7 @@
 
 
 def third_kernel(
-    scale, place, sums, upper_rows, weight_rows, momentum, gradient, inputs, new_momentum, new_basis, new_weight, activations
+    scale, place, side, sums, upper_rows, weight_rows, momentum, gradient, inputs, new_momentum, new_basis, new_weight, activations
 ):
     rows, width = weight_rows.shape
     rank = new_basis.shape[0]
@@ -143,7 +143,10 @@
     high, middle, low = three_parts(basis)
     under = jnp.concatenate([high, middle, high, middle, low, high], axis=0).astype(bf16)
     step = jnp.dot(turned[:, : 6 * rank], under, preferred_element_type=f32)
-    fresh = (weight_rows[...].astype(f32) + step).astype(bf16)
+    block = rows // 4
+    starts = [core * 2 * block + (at_x ^ side[0]) * block for at_x in range(2) for core in range(2)]
+    held = jnp.concatenate([weight_rows[pl.ds(pl.multiple_of(start, block), block), :] for start in starts], axis=0)
+    fresh = (held.astype(f32) + step).astype(bf16)
     result = jnp.dot(left_side, fresh, preferred_element_type=f32).astype(bf16)
     activations[...] = result[: inputs.shape[0]]
     new_weight[...] = result[inputs.shape[0] : inputs.shape[0] + 1]
@@ -178,7 +181,7 @@
     )(upper_rows)
 
 
-def third_call(scale, rank, place, sums, upper_rows, weight_rows, momentum, gradient, inputs):
+def third_call(scale, rank, place, side, sums, upper_rows, weight_rows, momentum, gradient, inputs):
     width = weight_rows.shape[1]
     return pl.pallas_call(
         functools.partial(third_kernel, scale),
@@ -188,11 +191,11 @@
             jax.ShapeDtypeStruct((1, width), bf16),
             jax.ShapeDtypeStruct((inputs.shape[0], width), bf16),
         ),
-        in_specs=[pl.BlockSpec(memory_space=pltpu.SMEM)] + [vmem] * 6,
+        in_specs=[pl.BlockSpec(memory_space=pltpu.SMEM)] * 2 + [vmem] * 6,
         out_specs=(vmem,) * 4,
         compiler_params=small_grant,
         name="third",
-    )(place, sums, upper_rows, weight_rows, momentum, gradient, inputs)
+    )(place, side, sums, upper_rows, weight_rows, momentum, gradient, inputs)
 
 
 def on_device(momentum, gradient, basis, weight, inputs):
@@ -203,15 +206,17 @@
     peers = lax.axis_size("tp")
     scale = step_size * math.sqrt(width * peers / rows)
     far = spread(first_call(zh, momentum, gradient, basis, weight), "zh")
-    near = spread(replicated(far, ("zl", "xl")), ("zl", "xl")).reshape(zl * xl * zh, 2, width + tail)
-    upper_rows = lax.all_gather(near[:, 0, :], "c", axis=0, tiled=True)
-    weight_rows = lax.all_gather(near[:, 1, :width], "c", axis=0, tiled=True)
+    near = spread(replicated(far, "zl"), "zl").reshape(zl * zh, 2, width + tail)
+    upper_rows = lax.all_gather(near[:, 0, :], ("xl", "c"), axis=0, tiled=True)
+    weight_near, upper_rows = lax.optimization_barrier((near[:, 1, :width], upper_rows))
+    across = lax.ppermute(weight_near, "xl", [(0, 1), (1, 0)])
     sums = spread(second_call(peers, rank, upper_rows), "tp")
-    place = ((lax.axis_index("c") * zl + lax.axis_index("zl")) * xl + lax.axis_index("xl")) * zh + lax.axis_index("zh")
-    ordered = inputs.reshape(-1, zh, zl, xl, c).transpose(0, 4, 2, 3, 1).reshape(-1, rows)
-    return third_call(
-        scale, rank, place.reshape(1).astype(jnp.int32), sums, upper_rows, weight_rows, momentum, gradient, ordered
-    )
+    weight_rows = lax.all_gather(jnp.concatenate([weight_near, across], axis=0), "c", axis=0, tiled=True)
+    at_x = lax.axis_index("xl")
+    place = ((at_x * c + lax.axis_index("c")) * zl + lax.axis_index("zl")) * zh + lax.axis_index("zh")
+    ordered = inputs.reshape(-1, zh, zl, xl, c).transpose(0, 3, 4, 2, 1).reshape(-1, rows)
+    place, side = (x.reshape(1).astype(jnp.int32) for x in (place, at_x))
+    return third_call(scale, rank, place, side, sums, upper_rows, weight_rows, momentum, gradient, ordered)
 
 
 def solution(mesh):

time: 107 us -> 106 us (level)
  blocking collectives: 87.8 us -> 83.9 us
  starting transfers between devices: 6.5 us -> 8.81 us
    all_to_all x2, blocking collectives: 80.4 us -> 69.4 us  [spread(): return lax.all_to_all(blocks, axes, 0, 0)]
    all_gather x2, blocking collectives: 7.45 us -> 14.5 us  [the longest x1 11.7 us: on_device(): upper_rows = lax.all_gather(near[:, 0, :], ('xl', 'c'), axis=0, tiled=True)]
    ppermute x0 -> x1, starting transfers between devices: none -> 2.15 us  [on_device(): across = lax.ppermute(weight_near, 'xl', [(0, 1), (1, 0)])]
  transfers between devices with their start and end apart: 1 -> 2, of which waited for: 1 -> 1; matrix products, arithmetic and copies ran while one was open for 0% -> 0% of each run, Pallas kernels for 0% -> 1%
where the time goes in v6:
time: 106 us; the launch traced here: 105 us
  blocking collectives  83.9 us (79%)
  starting transfers between devices  8.81 us (8%)
  waiting for transfers between devices  7.07 us (7%)
  Pallas kernels  4.5 us (4%)
    all_to_all x2, blocking collectives, spread(): return lax.all_to_all(blocks, axes, 0, 0)  69.4 us
    all_gather x1, blocking collectives, on_device(): upper_rows = lax.all_gather(near[:, 0, :], ('xl', 'c'), axis=0, tiled=True)  11.7 us
    all_to_all x1, waiting for transfers between devices, spread(): return lax.all_to_all(blocks, axes, 0, 0)  7.07 us
    all_to_all x1, starting transfers between devices, spread(): return lax.all_to_all(blocks, axes, 0, 0)  6.66 us
    all_gather x1, blocking collectives, on_device(): lax.all_gather(jnp.concatenate([weight_near, across], axis=0), 'c', axis=...  2.77 us
    pallas_call x1, Pallas kernels, third_call(): pl.pallas_call(functools.partial(third_kernel, scale), out_shape=(jax.Sha...  2.19 us
    ppermute x1, starting transfers between devices, on_device(): across = lax.ppermute(weight_near, 'xl', [(0, 1), (1, 0)])  2.15 us
  transfers between devices with their start and end apart: 2, of which 1 were waited for; matrix products, arithmetic and copies ran while one was open for 0% of the time, Pallas kernels for 1%

profile of v6, /device:TPU:1, one launch (start us, length us, event | category | flops | bytes accessed | tf_op | source)
XLA Modules:
  0.0 105.4 jit_solution(6154794144070138228)
XLA Ops:
  0.6 1.1 %first.1 = bf16[8,2,3456]{2,1,0:T(2,128)(2,1)S(1)} custom-call(f32[1,3328]{1,0:T(1,128)} %momentum.1, f32[1,3328]{1,0:T(1,128)} %gradient.1, f32[8,3328]{1,0:T(8,128)} %basis_hbm.1, bf16[1,3328]{1,0:T(2,128)(2,1)} %weight_hbm.1), custom_call_target="tpu_custom_call" | custom-call | tf_op jit(solution)/shard_map/first/pallas_call | solution.py:161
  1.7 52.2 %all_to_all.15 = bf16[8,2,3456]{2,1,0:T(2,128)(2,1)S(1)} all-to-all(bf16[8,2,3456]{2,1,0:T(2,128)(2,1)S(1)} %first.1), channel_id=1, replica_groups=mesh['zh'=8,'zl'=4,'xl'=2,'c'=2,'tp'=8] {'zh'}, dimensions={0} | all-to-all | bytes 221184 | tf_op jit(solution)/shard_map/all_to_all | solution.py:22
  54.0 17.2 %all_to_all.16 = bf16[4,8,2,3456]{3,1,2,0:T(8,128)(2,1)S(1)} all-to-all(bf16[4,8,2,3456]{3,1,2,0:T(8,128)(2,1)S(1)} %broadcast_in_dim.2), channel_id=1, replica_groups=mesh['zh'=8,'zl'=4,'xl'=2,'c'=2,'tp'=8] {'zl'}, dimensions={0} | all-to-all | bytes 884736 | tf_op jit(solution)/shard_map/all_to_all | solution.py:22
  71.3 0.0 copy-start.2
  71.3 11.7 %all-gather = bf16[128,1,3456]{2,0,1:T(8,128)(2,1)S(1)} all-gather(bf16[32,1,3456]{2,0,1:T(8,128)(2,1)S(1)} %slice.9), channel_id=2, replica_groups=mesh['zh'=8,'zl'=4,'xl'=2,'c'=2,'tp'=8] {'xl','c'}, dimensions={0}, use_global_device_ids=true | all-gather | bytes 1105920 | tf_op jit(solution)/shard_map/all_gather | solution.py:210
  83.0 2.2 %collective-permute-start = (bf16[32,3328]{1,0:T(8,128)(2,1)S(1)}, bf16[32,3328]{1,0:T(8,128)(2,1)S(1)}, u32[]{:S(2)}, u32[]{:S(2)}) collective-permute-start(bf16[32,3328]{1,0:T(8,128)(2,1)S(1)} %slice_bitcast_fusion), channel_id=1, source_target_pairs={{0,16},{16,0},{1,17},{17,1},{2,18},{18,2},{3,19},{19,3},{4,20},{20... | collective-permute-start | bytes 638984 | tf_op jit(solution)/shard_map/ppermute | solution.py:212
  85.2 0.0 copy-done.2
  85.2 0.1 copy.17
  85.3 0.1 copy.19.inputs
  85.4 1.2 %second.1 = f32[8,104,128]{2,1,0:T(8,128)} custom-call(bf16[128,3456]{1,0:T(8,128)(2,1)S(1)} %bitcast.12), custom_call_target="tpu_custom_call" | custom-call | tf_op jit(solution)/shard_map/second/pallas_call | solution.py:174
  86.7 6.7 %all-to-all-start.2 = ((f32[8,104,128]{2,1,0:T(8,128)}), f32[8,104,128]{2,1,0:T(8,128)S(1)}, u32[]{:S(2)}, u32[]{:S(2)}) async-start(f32[8,104,128]{2,1,0:T(8,128)} %second.1), calls=%async_computation.2 | async-start | bytes 851968 | tf_op jit(solution)/shard_map/all_to_all | solution.py:22
  93.3 0.0 collective-permute-done
  93.4 0.0 copy-start
  93.4 0.0 copy-start.1
  93.4 2.8 %all_gather.7.weight_rows = bf16[128,3328]{1,0:T(8,128)(2,1)S(1)} all-gather(bf16[64,3328]{1,0:T(8,128)(2,1)S(1)} %pad_maximum_fusion), channel_id=1, replica_groups=mesh['zh'=8,'zl'=4,'xl'=2,'c'=2,'tp'=8] {'c'}, dimensions={0}, use_global_device_ids=true | all-gather | bytes 1277952 | tf_op jit(solution)/shard_map/all_gather | solution.py:214
  96.2 7.1 %all-to-all-done.2.sums = f32[8,104,128]{2,1,0:T(8,128)S(1)} async-done(((f32[8,104,128]{2,1,0:T(8,128)}), f32[8,104,128]{2,1,0:T(8,128)S(1)}, u32[]{:S(2)}, u32[]{:S(2)}) %all-to-all-start.2) | async-done | bytes 426016 | tf_op jit(solution)/shard_map/all_to_all | solution.py:22
  103.2 0.0 copy-done
  103.2 0.0 copy-done.1
  103.2 2.2 %third.1 = (f32[1,3328]{1,0:T(1,128)}, f32[8,3328]{1,0:T(8,128)}, bf16[1,3328]{1,0:T(2,128)(2,1)}, bf16[128,3328]{1,0:T(8,128)(2,1)}) custom-call(s32[1]{0:T(128)} %bitcast.place, s32[1]{0:T(128)} %bitcast.1.side, f32[8,104,128]{2,1,0:T(8,128)S(1)} %all-to-all-done.2.sums, bf16[128,3456]{1,0:T(8,128)(2,1)S(1)} %bitcast.13, ...), custom_call_target="tpu_custom_call" | custom-call | tf_op jit(solution)/shard_map/third/pallas_call | solution.py:186
  (7 shorter events, 0.2 us)
Async XLA Ops:
  71.3 13.9 %copy-start.2 = (bf16[128,128]{1,0:T(8,128)(2,1)S(1)}, bf16[128,128]{1,0:T(8,128)(2,1)}, u32[]{:S(2)}) copy-start(bf16[128,128]{1,0:T(8,128)(2,1)} %param.9) | copy-start | bytes 98308
  83.0 10.3 %collective-permute-start = (bf16[32,3328]{1,0:T(8,128)(2,1)S(1)}, bf16[32,3328]{1,0:T(8,128)(2,1)S(1)}, u32[]{:S(2)}, u32[]{:S(2)}) collective-permute-start(bf16[32,3328]{1,0:T(8,128)(2,1)S(1)} %slice_bitcast_fusion), channel_id=1, source_target_pairs={{0,16},{16,0},{1,17},{17,1},{2,18},{18,2},{3,19},{19,3},{4,20},{20... | collective-permute-start | bytes 638984 | tf_op jit(solution)/shard_map/ppermute | solution.py:212
  86.7 16.6 %all-to-all-start.2 = ((f32[8,104,128]{2,1,0:T(8,128)}), f32[8,104,128]{2,1,0:T(8,128)S(1)}, u32[]{:S(2)}, u32[]{:S(2)}) async-start(f32[8,104,128]{2,1,0:T(8,128)} %second.1), calls=%async_computation.2 | async-start | bytes 851968 | tf_op jit(solution)/shard_map/all_to_all | solution.py:22
  93.4 9.9 %copy-start = (f32[1,3328]{1,0:T(1,128)S(1)}, f32[1,3328]{1,0:T(1,128)}, u32[]{:S(2)}) copy-start(f32[1,3328]{1,0:T(1,128)} %momentum.1) | copy-start | bytes 39940
  93.4 9.9 %copy-start.1 = (f32[1,3328]{1,0:T(1,128)S(1)}, f32[1,3328]{1,0:T(1,128)}, u32[]{:S(2)}) copy-start(f32[1,3328]{1,0:T(1,128)} %gradient.1) | copy-start | bytes 39940

commit v7 on v6

--- a/solution.py
+++ b/solution.py
@@ -7,6 +7,7 @@
 from jax.experimental import pallas as pl
 from jax.experimental.pallas import tpu as pltpu
 from jax.sharding import Mesh, PartitionSpec as P
+
 
 decay_rate = 0.8
 step_size = 0.5
@@ -208,9 +209,10 @@
     far = spread(first_call(zh, momentum, gradient, basis, weight), "zh")
     near = spread(replicated(far, "zl"), "zl").reshape(zl * zh, 2, width + tail)
     upper_rows = lax.all_gather(near[:, 0, :], ("xl", "c"), axis=0, tiled=True)
-    weight_near, upper_rows = lax.optimization_barrier((near[:, 1, :width], upper_rows))
+    weight_near = near[:, 1, :width]
+    blocks = second_call(peers, rank, upper_rows)
+    sums = spread(blocks, "tp")
     across = lax.ppermute(weight_near, "xl", [(0, 1), (1, 0)])
-    sums = spread(second_call(peers, rank, upper_rows), "tp")
     weight_rows = lax.all_gather(jnp.concatenate([weight_near, across], axis=0), "c", axis=0, tiled=True)
     at_x = lax.axis_index("xl")
     place = ((at_x * c + lax.axis_index("c")) * zl + lax.axis_index("zl")) * zh + lax.axis_index("zh")

time: 106 us -> 109 us (1.028)
  blocking collectives: 83.9 us -> 68.5 us
  waiting for transfers between devices: 7.07 us -> 17.1 us
  starting transfers between devices: 8.81 us -> 16.3 us
    all_to_all x2 -> x1, blocking collectives: 69.4 us -> 52.2 us  [spread(): return lax.all_to_all(blocks, axes, 0, 0)]
    all_to_all x1 -> x2, waiting for transfers between devices: 7.07 us -> 17.1 us  [spread(): return lax.all_to_all(blocks, axes, 0, 0)]
    all_to_all x1 -> x2, starting transfers between devices: 6.66 us -> 13.2 us  [spread(): return lax.all_to_all(blocks, axes, 0, 0)]
    all_gather x1, blocking collectives: 11.7 us -> 13.8 us  [on_device(): upper_rows = lax.all_gather(near[:, 0, :], ('xl', 'c'), axis=0, tiled=True)]
  transfers between devices with their start and end apart: 2 -> 3, of which waited for: 1 -> 2; matrix products, arithmetic and copies ran while one was open for 0% -> 0% of each run, Pallas kernels for 1% -> 1%
where the time goes in v7:
time: 109 us; the launch traced here: 108 us
  blocking collectives  68.5 us (63%)
  waiting for transfers between devices  17.1 us (16%)
  starting transfers between devices  16.3 us (15%)
  Pallas kernels  4.51 us (4%)
  local copies, waits for them, and re-layouts  1.12 us (1%)
    all_to_all x1, blocking collectives, spread(): return lax.all_to_all(blocks, axes, 0, 0)  52.2 us
    all_to_all x2, waiting for transfers between devices, spread(): return lax.all_to_all(blocks, axes, 0, 0)  17.1 us
    all_gather x1, blocking collectives, on_device(): upper_rows = lax.all_gather(near[:, 0, :], ('xl', 'c'), axis=0, tiled=True)  13.8 us
    all_to_all x2, starting transfers between devices, spread(): return lax.all_to_all(blocks, axes, 0, 0)  13.2 us
    ppermute x1, starting transfers between devices, on_device(): across = lax.ppermute(weight_near, 'xl', [(0, 1), (1, 0)])  3.12 us
    all_gather x1, blocking collectives, on_device(): lax.all_gather(jnp.concatenate([weight_near, across], axis=0), 'c', axis=...  2.49 us
    pallas_call x1, Pallas kernels, third_call(): pl.pallas_call(functools.partial(third_kernel, scale), out_shape=(jax.Sha...  2.19 us
  transfers between devices with their start and end apart: 3, of which 2 were waited for; matrix products, arithmetic and copies ran while one was open for 0% of the time, Pallas kernels for 1%

profile of v7, /device:TPU:1, one launch (start us, length us, event | category | flops | bytes accessed | tf_op | source)
XLA Modules:
  0.0 108.4 jit_solution(964173204644419873)
XLA Ops:
  0.6 1.1 %first.1 = bf16[8,2,3456]{2,1,0:T(2,128)(2,1)S(1)} custom-call(f32[1,3328]{1,0:T(1,128)} %momentum.1, f32[1,3328]{1,0:T(1,128)} %gradient.1, f32[8,3328]{1,0:T(8,128)} %basis_hbm.1, bf16[1,3328]{1,0:T(2,128)(2,1)} %weight_hbm.1), custom_call_target="tpu_custom_call" | custom-call | tf_op jit(solution)/shard_map/first/pallas_call | solution.py:162
  1.7 52.2 %all_to_all.15 = bf16[8,2,3456]{2,1,0:T(2,128)(2,1)S(1)} all-to-all(bf16[8,2,3456]{2,1,0:T(2,128)(2,1)S(1)} %first.1), channel_id=1, replica_groups=mesh['zh'=8,'zl'=4,'xl'=2,'c'=2,'tp'=8] {'zh'}, dimensions={0} | all-to-all | bytes 221184 | tf_op jit(solution)/shard_map/all_to_all | solution.py:23
  54.0 0.8 broadcast_in_dim.2
  54.7 0.0 copy-start.2
  54.7 6.6 %all-to-all-start.1 = ((bf16[4,8,2,3456]{3,1,2,0:T(8,128)(2,1)}), bf16[4,8,2,3456]{3,1,2,0:T(8,128)(2,1)S(1)}, u32[]{:S(2)}, u32[]{:S(2)}) async-start(bf16[4,8,2,3456]{3,1,2,0:T(8,128)(2,1)} %broadcast_in_dim.2), calls=%async_computation.1 | async-start | bytes 884736 | tf_op jit(solution)/shard_map/all_to_all | solution.py:23
  61.3 0.0 copy-done.2
  61.3 0.1 copy.17
  61.5 0.1 copy.19.inputs
  61.6 9.7 %all-to-all-done.1 = bf16[4,8,2,3456]{3,1,2,0:T(8,128)(2,1)S(1)} async-done(((bf16[4,8,2,3456]{3,1,2,0:T(8,128)(2,1)}), bf16[4,8,2,3456]{3,1,2,0:T(8,128)(2,1)S(1)}, u32[]{:S(2)}, u32[]{:S(2)}) %all-to-all-start.1) | async-done | bytes 442400 | tf_op jit(solution)/shard_map/all_to_all | solution.py:23
  71.4 3.1 %collective-permute-start = (bf16[32,3328]{1,0:T(8,128)(2,1)S(1)}, bf16[32,3328]{1,0:T(8,128)(2,1)S(1)}, u32[]{:S(2)}, u32[]{:S(2)}) collective-permute-start(bf16[32,3328]{1,0:T(8,128)(2,1)S(1)} %slice_bitcast_fusion), channel_id=1, source_target_pairs={{0,16},{16,0},{1,17},{17,1},{2,18},{18,2},{3,19},{19,3},{4,20},{20... | collective-permute-start | bytes 638984 | tf_op jit(solution)/shard_map/ppermute | solution.py:215
  74.5 13.8 %all-gather = bf16[128,1,3456]{2,0,1:T(8,128)(2,1)S(1)} all-gather(bf16[32,1,3456]{2,0,1:T(8,128)(2,1)S(1)} %slice.8), channel_id=2, replica_groups=mesh['zh'=8,'zl'=4,'xl'=2,'c'=2,'tp'=8] {'xl','c'}, dimensions={0}, use_global_device_ids=true | all-gather | bytes 1105920 | tf_op jit(solution)/shard_map/all_gather | solution.py:211
  88.3 1.2 %second.1 = f32[8,104,128]{2,1,0:T(8,128)} custom-call(bf16[128,3456]{1,0:T(8,128)(2,1)S(1)} %bitcast.12), custom_call_target="tpu_custom_call" | custom-call | tf_op jit(solution)/shard_map/second/pallas_call | solution.py:175
  89.5 6.6 %all-to-all-start.2 = ((f32[8,104,128]{2,1,0:T(8,128)}), f32[8,104,128]{2,1,0:T(8,128)S(1)}, u32[]{:S(2)}, u32[]{:S(2)}) async-start(f32[8,104,128]{2,1,0:T(8,128)} %second.1), calls=%async_computation.2 | async-start | bytes 851968 | tf_op jit(solution)/shard_map/all_to_all | solution.py:23
  96.2 0.0 collective-permute-done
  96.2 0.0 copy-start
  96.2 0.0 copy-start.1
  96.2 2.5 %all_gather.7.weight_rows = bf16[128,3328]{1,0:T(8,128)(2,1)S(1)} all-gather(bf16[64,3328]{1,0:T(8,128)(2,1)S(1)} %pad_maximum_fusion), channel_id=1, replica_groups=mesh['zh'=8,'zl'=4,'xl'=2,'c'=2,'tp'=8] {'c'}, dimensions={0}, use_global_device_ids=true | all-gather | bytes 1277952 | tf_op jit(solution)/shard_map/all_gather | solution.py:216
  98.7 7.4 %all-to-all-done.2.sums = f32[8,104,128]{2,1,0:T(8,128)S(1)} async-done(((f32[8,104,128]{2,1,0:T(8,128)}), f32[8,104,128]{2,1,0:T(8,128)S(1)}, u32[]{:S(2)}, u32[]{:S(2)}) %all-to-all-start.2) | async-done | bytes 426016 | tf_op jit(solution)/shard_map/all_to_all | solution.py:23
  106.2 0.0 copy-done
  106.2 0.0 copy-done.1
  106.2 2.2 %third.1 = (f32[1,3328]{1,0:T(1,128)}, f32[8,3328]{1,0:T(8,128)}, bf16[1,3328]{1,0:T(2,128)(2,1)}, bf16[128,3328]{1,0:T(8,128)(2,1)}) custom-call(s32[1]{0:T(128)} %bitcast.place, s32[1]{0:T(128)} %bitcast.1.side, f32[8,104,128]{2,1,0:T(8,128)S(1)} %all-to-all-done.2.sums, bf16[128,3456]{1,0:T(8,128)(2,1)S(1)} %bitcast.13, ...), custom_call_target="tpu_custom_call" | custom-call | tf_op jit(solution)/shard_map/third/pallas_call | solution.py:187
  (6 shorter events, 0.1 us)
Async XLA Ops:
  54.7 6.6 %copy-start.2 = (bf16[128,128]{1,0:T(8,128)(2,1)S(1)}, bf16[128,128]{1,0:T(8,128)(2,1)}, u32[]{:S(2)}) copy-start(bf16[128,128]{1,0:T(8,128)(2,1)} %param.9) | copy-start | bytes 98308
  54.7 16.5 %all-to-all-start.1 = ((bf16[4,8,2,3456]{3,1,2,0:T(8,128)(2,1)}), bf16[4,8,2,3456]{3,1,2,0:T(8,128)(2,1)S(1)}, u32[]{:S(2)}, u32[]{:S(2)}) async-start(bf16[4,8,2,3456]{3,1,2,0:T(8,128)(2,1)} %broadcast_in_dim.2), calls=%async_computation.1 | async-start | bytes 884736 | tf_op jit(solution)/shard_map/all_to_all | solution.py:23
  71.4 24.8 %collective-permute-start = (bf16[32,3328]{1,0:T(8,128)(2,1)S(1)}, bf16[32,3328]{1,0:T(8,128)(2,1)S(1)}, u32[]{:S(2)}, u32[]{:S(2)}) collective-permute-start(bf16[32,3328]{1,0:T(8,128)(2,1)S(1)} %slice_bitcast_fusion), channel_id=1, source_target_pairs={{0,16},{16,0},{1,17},{17,1},{2,18},{18,2},{3,19},{19,3},{4,20},{20... | collective-permute-start | bytes 638984 | tf_op jit(solution)/shard_map/ppermute | solution.py:215
  89.5 16.6 %all-to-all-start.2 = ((f32[8,104,128]{2,1,0:T(8,128)}), f32[8,104,128]{2,1,0:T(8,128)S(1)}, u32[]{:S(2)}, u32[]{:S(2)}) async-start(f32[8,104,128]{2,1,0:T(8,128)} %second.1), calls=%async_computation.2 | async-start | bytes 851968 | tf_op jit(solution)/shard_map/all_to_all | solution.py:23
  96.2 10.0 %copy-start = (f32[1,3328]{1,0:T(1,128)S(1)}, f32[1,3328]{1,0:T(1,128)}, u32[]{:S(2)}) copy-start(f32[1,3328]{1,0:T(1,128)} %momentum.1) | copy-start | bytes 39940
  96.2 10.0 %copy-start.1 = (f32[1,3328]{1,0:T(1,128)S(1)}, f32[1,3328]{1,0:T(1,128)}, u32[]{:S(2)}) copy-start(f32[1,3328]{1,0:T(1,128)} %gradient.1) | copy-start | bytes 39940

commit v8 on v5

--- a/solution.py
+++ b/solution.py
@@ -73,35 +73,52 @@
 def second_kernel(upper_rows, out):
     rows = upper_rows.shape[0]
     width = upper_rows.shape[1] - tail
-    half, quarter = rows // 2, rows // 4
-    rank = out.shape[1] - half - quarter
+    half, quarter, eighth = rows // 2, rows // 4, rows // 8
+    rank = out.shape[1] - half - eighth
     buffer = upper_rows[:, :width]
     square = lax.dot_general(buffer, buffer, (((1,), (1,)), ((), ())), preferred_element_type=f32)
     corner = pltpu.roll(square[half + quarter :], quarter, 1)
-    folded = jnp.where(iota((quarter, rows), 1) < quarter, corner, square[half : half + quarter])
+    inner = jnp.where(iota((quarter, rows), 1) < quarter, corner, square[quarter:half])
+    moved = pltpu.roll(square[half + eighth : half + quarter], half, 1)
+    last = jnp.where(iota((eighth, rows), 1) < half, moved, square[half : half + eighth])
     coded = upper_rows[:, width:].astype(f32).T
     power = coded[:rank] + coded[rank : 2 * rank] + coded[2 * rank : 3 * rank]
     for peer in range(out.shape[0]):
-        out[peer, :half] = square[:half]
-        out[peer, half : half + quarter] = folded
-        out[peer, half + quarter :] = power
+        out[peer, :quarter] = square[:quarter]
+        out[peer, quarter:half] = inner
+        out[peer, half : half + eighth] = last
+        out[peer, half + eighth :] = power
 
 
 def quadratic(folded, vectors):
     rank, rows = vectors.shape
-    half, quarter = rows // 2, rows // 4
+    half, quarter, eighth = rows // 2, rows // 4, rows // 8
     lane = iota((rank, rows), 1)
-    in_third = (lane >= half) & (lane < half + quarter)
-    turned = pltpu.roll(vectors, rows - quarter, 1)
+
+    def within(low, high, values):
+        return jnp.where((lane >= low) & (lane < high), values, 0.0)
+
+    def weights(start, single):
+        return jnp.where(lane < start, 0.0, jnp.where(lane < single, 1.0, 2.0))
+
+    by_quarter, by_half = pltpu.roll(vectors, quarter, 1), pltpu.roll(vectors, half, 1)
     left = jnp.concatenate(
-        [jnp.where(lane < half, vectors, 0.0), jnp.where(in_third, vectors, 0.0), jnp.where(in_third, turned, 0.0)], axis=0
+        [
+            within(0, quarter, vectors),
+            within(quarter, half, vectors),
+            within(quarter, half, by_half),
+            within(half, half + eighth, vectors),
+            within(half, half + eighth, pltpu.roll(vectors, rows - eighth, 1)),
+        ],
+        axis=0,
     )
-    right = jnp.concatenate([folded, jnp.zeros((quarter, rows), f32)], axis=0)
+    right = jnp.concatenate([folded, jnp.zeros((rows - half - eighth, rows), f32)], axis=0)
     along = lax.dot_general(left, right, (((1,), (0,)), ((), ())), precision=highest, preferred_element_type=f32)
-    top = along[:rank] * vectors * jnp.where(lane < half, 1.0, 2.0)
-    middle = along[rank : 2 * rank] * vectors * jnp.where(lane < half, 0.0, jnp.where(lane < half + quarter, 1.0, 2.0))
-    corner = jnp.where(lane < quarter, along[2 * rank :] * pltpu.roll(vectors, quarter, 1), 0.0)
-    return jnp.sum(top + middle + corner, axis=1, keepdims=True)
+    first, second, third, fourth, fifth = (along[n * rank : (n + 1) * rank] for n in range(5))
+    plain = first * weights(0, quarter) + second * weights(quarter, half) + fourth * weights(half, half + quarter)
+    total = plain * vectors + within(0, quarter, third) * by_quarter
+    total = total + within(0, half, fifth * weights(0, quarter)) * by_half
+    return jnp.sum(total, axis=1, keepdims=True)
 
 
 def third_kernel(
@@ -170,7 +187,7 @@
     rows = upper_rows.shape[0]
     return pl.pallas_call(
         second_kernel,
-        out_shape=jax.ShapeDtypeStruct((peers, rows // 2 + rows // 4 + rank, rows), f32),
+        out_shape=jax.ShapeDtypeStruct((peers, rows // 2 + rows // 8 + rank, rows), f32),
         in_specs=[vmem],
         out_specs=vmem,
         compiler_params=small_grant,

time: 105 us -> 105 us (level)
  blocking collectives: 92.4 us -> 75.8 us
  waiting for transfers between devices: 0.01 us -> 9.7 us
  starting transfers between devices: 6.48 us -> 12.9 us
    all_to_all x2 -> x1, blocking collectives: 69.4 us -> 52.2 us  [spread(): return lax.all_to_all(blocks, axes, 0, 0)]
    all_to_all x1 -> x2, waiting for transfers between devices: 0.01 us -> 9.7 us  [spread(): return lax.all_to_all(blocks, axes, 0, 0)]
    all_to_all x1 -> x2, starting transfers between devices: 6.48 us -> 12.9 us  [spread(): return lax.all_to_all(blocks, axes, 0, 0)]
  transfers between devices with their start and end apart: 1 -> 2, of which waited for: 0 -> 1; matrix products, arithmetic and copies ran while one was open for 0% -> 0% of each run, Pallas kernels for 0% -> 0%
where the time goes in v8:
time: 105 us
  blocking collectives  75.8 us (72%)
  starting transfers between devices  12.9 us (12%)
  waiting for transfers between devices  9.7 us (9%)
  Pallas kernels  4.51 us (4%)
  local copies, waits for them, and re-layouts  1.12 us (1%)
    all_to_all x1, blocking collectives, spread(): return lax.all_to_all(blocks, axes, 0, 0)  52.2 us
    all_to_all x2, starting transfers between devices, spread(): return lax.all_to_all(blocks, axes, 0, 0)  12.9 us
    all_gather x1, blocking collectives, on_device(): upper_rows = lax.all_gather(near[:, 0, :], 'a', axis=0, tiled=True)  12.7 us
    all_gather x1, blocking collectives, on_device(): weight_rows = lax.all_gather(near[:, 1, :width], 'a', axis=0, tiled=True)  10.9 us
    all_to_all x2, waiting for transfers between devices, spread(): return lax.all_to_all(blocks, axes, 0, 0)  9.7 us
    pallas_call x1, Pallas kernels, third_call(): pl.pallas_call(functools.partial(third_kernel, scale), out_shape=(jax.Sha...  2.21 us
  transfers between devices with their start and end apart: 2, of which 1 were waited for; matrix products, arithmetic and copies ran while one was open for 0% of the time, Pallas kernels for 0%

profile of v8, /device:TPU:1, one launch (start us, length us, event | category | flops | bytes accessed | tf_op | source)
XLA Modules:
  0.0 104.8 jit_solution(8124898432843150124)
XLA Ops:
  0.6 1.1 %first.1 = bf16[8,2,3456]{2,1,0:T(2,128)(2,1)S(1)} custom-call(f32[1,3328]{1,0:T(1,128)} %momentum.1, f32[1,3328]{1,0:T(1,128)} %gradient.1, f32[8,3328]{1,0:T(8,128)} %basis_hbm.1, bf16[1,3328]{1,0:T(2,128)(2,1)} %weight_hbm.1), custom_call_target="tpu_custom_call" | custom-call | tf_op jit(solution)/shard_map/first/pallas_call | solution.py:175
  1.7 52.2 %all_to_all.15 = bf16[8,2,3456]{2,1,0:T(2,128)(2,1)S(1)} all-to-all(bf16[8,2,3456]{2,1,0:T(2,128)(2,1)S(1)} %first.1), channel_id=1, replica_groups=mesh['zh'=8,'zl'=4,'a'=4,'tp'=8] {'zh'}, dimensions={0} | all-to-all | bytes 221184 | tf_op jit(solution)/shard_map/all_to_all | solution.py:22
  54.0 0.8 broadcast_in_dim.2
  54.7 0.0 copy-start.2
  54.7 6.6 %all-to-all-start.1 = ((bf16[4,8,2,3456]{3,1,2,0:T(8,128)(2,1)}), bf16[4,8,2,3456]{3,1,2,0:T(8,128)(2,1)S(1)}, u32[]{:S(2)}, u32[]{:S(2)}) async-start(bf16[4,8,2,3456]{3,1,2,0:T(8,128)(2,1)} %broadcast_in_dim.2), calls=%async_computation.1 | async-start | bytes 884736 | tf_op jit(solution)/shard_map/all_to_all | solution.py:22
  61.3 0.0 copy-done.2
  61.3 0.1 copy.17
  61.5 0.1 copy.19.inputs
  61.6 9.7 %all-to-all-done.1 = bf16[4,8,2,3456]{3,1,2,0:T(8,128)(2,1)S(1)} async-done(((bf16[4,8,2,3456]{3,1,2,0:T(8,128)(2,1)}), bf16[4,8,2,3456]{3,1,2,0:T(8,128)(2,1)S(1)}, u32[]{:S(2)}, u32[]{:S(2)}) %all-to-all-start.1) | async-done | bytes 442400 | tf_op jit(solution)/shard_map/all_to_all | solution.py:22
  71.4 12.7 %all-gather = bf16[128,1,3456]{2,0,1:T(8,128)(2,1)S(1)} all-gather(bf16[32,1,3456]{2,0,1:T(8,128)(2,1)S(1)} %slice.8), channel_id=2, replica_groups=mesh['zh'=8,'zl'=4,'a'=4,'tp'=8] {'a'}, dimensions={0}, use_global_device_ids=true | all-gather | bytes 1105920 | tf_op jit(solution)/shard_map/all_gather | solution.py:224
  84.1 1.2 %second.1 = f32[8,88,128]{2,1,0:T(8,128)} custom-call(bf16[128,3456]{1,0:T(8,128)(2,1)S(1)} %bitcast.10), custom_call_target="tpu_custom_call" | custom-call | tf_op jit(solution)/shard_map/second/pallas_call | solution.py:188
  85.3 6.4 %all-to-all-start.2 = ((f32[8,88,128]{2,1,0:T(8,128)}), f32[8,88,128]{2,1,0:T(8,128)S(1)}, u32[]{:S(2)}, u32[]{:S(2)}) async-start(f32[8,88,128]{2,1,0:T(8,128)} %second.1), calls=%async_computation.2 | async-start | bytes 720896 | tf_op jit(solution)/shard_map/all_to_all | solution.py:22
  91.6 0.0 copy-start
  91.6 0.0 copy-start.1
  91.6 10.9 %all-gather.1 = bf16[128,1,3328]{2,0,1:T(8,128)(2,1)S(1)} all-gather(bf16[32,1,3328]{2,0,1:T(8,128)(2,1)S(1)} %slice.9), channel_id=3, replica_groups=mesh['zh'=8,'zl'=4,'a'=4,'tp'=8] {'a'}, dimensions={0}, use_global_device_ids=true | all-gather | bytes 1064960 | tf_op jit(solution)/shard_map/all_gather | solution.py:225
  102.6 0.0 all-to-all-done.2.sums
  102.6 0.0 copy-done
  102.6 0.0 copy-done.1
  102.6 2.2 %third.1 = (f32[1,3328]{1,0:T(1,128)}, f32[8,3328]{1,0:T(8,128)}, bf16[1,3328]{1,0:T(2,128)(2,1)}, bf16[128,3328]{1,0:T(8,128)(2,1)}) custom-call(s32[1]{0:T(128)} %bitcast.place, f32[8,88,128]{2,1,0:T(8,128)S(1)} %all-to-all-done.2.sums, bf16[128,3456]{1,0:T(8,128)(2,1)S(1)} %bitcast.11, bf16[128,3328]{1,0:T(8,128)(2,1)S(1)} %bitcast.12, ...), custom_call_target="tpu_custom_call" | custom-call | tf_op jit(solution)/shard_map/third/pallas_call | solution.py:200
  (5 shorter events, 0.1 us)
Async XLA Ops:
  54.7 6.6 %copy-start.2 = (bf16[128,128]{1,0:T(8,128)(2,1)S(1)}, bf16[128,128]{1,0:T(8,128)(2,1)}, u32[]{:S(2)}) copy-start(bf16[128,128]{1,0:T(8,128)(2,1)} %param.9) | copy-start | bytes 98308
  54.7 16.5 %all-to-all-start.1 = ((bf16[4,8,2,3456]{3,1,2,0:T(8,128)(2,1)}), bf16[4,8,2,3456]{3,1,2,0:T(8,128)(2,1)S(1)}, u32[]{:S(2)}, u32[]{:S(2)}) async-start(bf16[4,8,2,3456]{3,1,2,0:T(8,128)(2,1)} %broadcast_in_dim.2), calls=%async_computation.1 | async-start | bytes 884736 | tf_op jit(solution)/shard_map/all_to_all | solution.py:22
  85.3 17.3 %all-to-all-start.2 = ((f32[8,88,128]{2,1,0:T(8,128)}), f32[8,88,128]{2,1,0:T(8,128)S(1)}, u32[]{:S(2)}, u32[]{:S(2)}) async-start(f32[8,88,128]{2,1,0:T(8,128)} %second.1), calls=%async_computation.2 | async-start | bytes 720896 | tf_op jit(solution)/shard_map/all_to_all | solution.py:22
  91.6 10.9 %copy-start = (f32[1,3328]{1,0:T(1,128)S(1)}, f32[1,3328]{1,0:T(1,128)}, u32[]{:S(2)}) copy-start(f32[1,3328]{1,0:T(1,128)} %momentum.1) | copy-start | bytes 39940
  91.6 10.9 %copy-start.1 = (f32[1,3328]{1,0:T(1,128)S(1)}, f32[1,3328]{1,0:T(1,128)}, u32[]{:S(2)}) copy-start(f32[1,3328]{1,0:T(1,128)} %gradient.1) | copy-start | bytes 39940

commit v9 on v8

--- a/solution.py
+++ b/solution.py
@@ -122,7 +122,7 @@
 
 
 def third_kernel(
-    scale, place, sums, upper_rows, weight_rows, momentum, gradient, inputs, new_momentum, new_basis, new_weight, activations
+    scale, sums, upper_rows, weight_rows, momentum, gradient, inputs, new_momentum, new_basis, new_weight, activations
 ):
     rows, width = weight_rows.shape
     rank = new_basis.shape[0]
@@ -147,7 +147,8 @@
     high, middle, low = three_parts(-scale * ortho)
     right_side = jnp.concatenate([high, high, middle, middle, high, low], axis=0)
     turned = jnp.concatenate([right_side, jnp.zeros((rows - 6 * rank, rows), f32)], axis=0).T.astype(bf16)
-    here = place[0]
+    zh, zl = lax.axis_size("zh"), lax.axis_size("zl")
+    here = (lax.axis_index("a") * zl + lax.axis_index("zl")) * zh + lax.axis_index("zh")
     own = jnp.sum(jnp.where(iota((rank, rows), 1) == here, ortho, 0.0), axis=1, keepdims=True) * (1.0 - decay_rate)
     chosen = (iota((16, rows), 1) == here).astype(f32).astype(bf16)
     left_side = jnp.concatenate([inputs[...], chosen], axis=0)
@@ -195,7 +196,7 @@
     )(upper_rows)
 
 
-def third_call(scale, rank, place, sums, upper_rows, weight_rows, momentum, gradient, inputs):
+def third_call(scale, rank, sums, upper_rows, weight_rows, momentum, gradient, inputs):
     width = weight_rows.shape[1]
     return pl.pallas_call(
         functools.partial(third_kernel, scale),
@@ -205,11 +206,11 @@
             jax.ShapeDtypeStruct((1, width), bf16),
             jax.ShapeDtypeStruct((inputs.shape[0], width), bf16),
         ),
-        in_specs=[pl.BlockSpec(memory_space=pltpu.SMEM)] + [vmem] * 6,
+        in_specs=[vmem] * 6,
         out_specs=(vmem,) * 4,
         compiler_params=small_grant,
         name="third",
-    )(place, sums, upper_rows, weight_rows, momentum, gradient, inputs)
+    )(sums, upper_rows, weight_rows, momentum, gradient, inputs)
 
 
 def on_device(momentum, gradient, basis, weight, inputs):
@@ -223,12 +224,10 @@
     near = spread(replicated(far, "zl"), "zl").reshape(zl * zh, 2, width + tail)
     upper_rows = lax.all_gather(near[:, 0, :], "a", axis=0, tiled=True)
     weight_rows = lax.all_gather(near[:, 1, :width], "a", axis=0, tiled=True)
-    sums = spread(second_call(peers, rank, upper_rows), "tp")
-    place = (lax.axis_index("a") * zl + lax.axis_index("zl")) * zh + lax.axis_index("zh")
+    inputs, blocks = lax.optimization_barrier((inputs, second_call(peers, rank, upper_rows)))
+    sums = spread(blocks, "tp")
     ordered = inputs.reshape(-1, zh, zl, a).transpose(0, 3, 2, 1).reshape(-1, rows)
-    return third_call(
-        scale, rank, place.reshape(1).astype(jnp.int32), sums, upper_rows, weight_rows, momentum, gradient, ordered
-    )
+    return third_call(scale, rank, sums, upper_rows, weight_rows, momentum, gradient, ordered)
 
 
 def solution(mesh):

time: 105 us -> 104 us (level)
  blocking collectives: 75.8 us -> 91.7 us
  waiting for transfers between devices: 9.7 us -> 0.01 us
  starting transfers between devices: 12.9 us -> 6.49 us
    all_to_all x1 -> x2, blocking collectives: 52.2 us -> 69.4 us  [spread(): return lax.all_to_all(blocks, axes, 0, 0)]
    all_to_all x2 -> x1, waiting for transfers between devices: 9.7 us -> 0.01 us  [spread(): return lax.all_to_all(blocks, axes, 0, 0)]
    all_to_all x2 -> x1, starting transfers between devices: 12.9 us -> 6.49 us  [spread(): return lax.all_to_all(blocks, axes, 0, 0)]
  transfers between devices with their start and end apart: 2 -> 1, of which waited for: 1 -> 0; matrix products, arithmetic and copies ran while one was open for 0% -> 0% of each run, Pallas kernels for 0% -> 0%
where the time goes in v9:
time: 104 us
  blocking collectives  91.7 us (88%)
  starting transfers between devices  6.49 us (6%)
  Pallas kernels  4.51 us (4%)
    all_to_all x2, blocking collectives, spread(): return lax.all_to_all(blocks, axes, 0, 0)  69.4 us
    all_gather x1, blocking collectives, on_device(): upper_rows = lax.all_gather(near[:, 0, :], 'a', axis=0, tiled=True)  11.7 us
    all_gather x1, blocking collectives, on_device(): weight_rows = lax.all_gather(near[:, 1, :width], 'a', axis=0, tiled=True)  10.6 us
    all_to_all x1, starting transfers between devices, spread(): return lax.all_to_all(blocks, axes, 0, 0)  6.49 us
    pallas_call x1, Pallas kernels, third_call(): pl.pallas_call(functools.partial(third_kernel, scale), out_shape=(jax.Sha...  2.2 us
  transfers between devices with their start and end apart: 1, of which 0 were waited for; matrix products, arithmetic and copies ran while one was open for 0% of the time, Pallas kernels for 0%

profile of v9, /device:TPU:1, one launch (start us, length us, event | category | flops | bytes accessed | tf_op | source)
XLA Modules:
  0.0 103.8 jit_solution(1934203612217675457)
XLA Ops:
  0.6 1.1 %first.1 = bf16[8,2,3456]{2,1,0:T(2,128)(2,1)S(1)} custom-call(f32[1,3328]{1,0:T(1,128)} %momentum.1, f32[1,3328]{1,0:T(1,128)} %gradient.1, f32[8,3328]{1,0:T(8,128)} %basis_hbm.1, bf16[1,3328]{1,0:T(2,128)(2,1)} %weight_hbm.1), custom_call_target="tpu_custom_call" | custom-call | tf_op jit(solution)/shard_map/first/pallas_call | solution.py:176
  1.7 52.2 %all_to_all.15 = bf16[8,2,3456]{2,1,0:T(2,128)(2,1)S(1)} all-to-all(bf16[8,2,3456]{2,1,0:T(2,128)(2,1)S(1)} %first.1), channel_id=1, replica_groups=mesh['zh'=8,'zl'=4,'a'=4,'tp'=8] {'zh'}, dimensions={0} | all-to-all | bytes 221184 | tf_op jit(solution)/shard_map/all_to_all | solution.py:22
  54.0 17.2 %all_to_all.16 = bf16[4,8,2,3456]{3,1,2,0:T(8,128)(2,1)S(1)} all-to-all(bf16[4,8,2,3456]{3,1,2,0:T(8,128)(2,1)S(1)} %broadcast_in_dim.2), channel_id=1, replica_groups=mesh['zh'=8,'zl'=4,'a'=4,'tp'=8] {'zl'}, dimensions={0} | all-to-all | bytes 884736 | tf_op jit(solution)/shard_map/all_to_all | solution.py:22
  71.3 11.7 %all-gather = bf16[128,1,3456]{2,0,1:T(8,128)(2,1)S(1)} all-gather(bf16[32,1,3456]{2,0,1:T(8,128)(2,1)S(1)} %slice.8), channel_id=2, replica_groups=mesh['zh'=8,'zl'=4,'a'=4,'tp'=8] {'a'}, dimensions={0}, use_global_device_ids=true | all-gather | bytes 1105920 | tf_op jit(solution)/shard_map/all_gather | solution.py:225
  83.0 1.2 %second.1 = f32[8,88,128]{2,1,0:T(8,128)} custom-call(bf16[128,3456]{1,0:T(8,128)(2,1)S(1)} %bitcast.9), custom_call_target="tpu_custom_call" | custom-call | tf_op jit(solution)/shard_map/second/pallas_call | solution.py:189
  84.2 0.0 copy-start.2
  84.2 6.5 %all-to-all-start.2 = ((f32[8,88,128]{2,1,0:T(8,128)}), f32[8,88,128]{2,1,0:T(8,128)S(1)}, u32[]{:S(2)}, u32[]{:S(2)}) async-start(f32[8,88,128]{2,1,0:T(8,128)} %second.1), calls=%async_computation.2 | async-start | bytes 720896 | tf_op jit(solution)/shard_map/all_to_all | solution.py:22
  90.7 0.0 copy-done.2
  90.7 0.1 copy.17
  90.8 0.1 copy.19.inputs
  90.9 0.0 copy-start
  90.9 0.0 copy-start.1
  91.0 10.6 %all-gather.1 = bf16[128,1,3328]{2,0,1:T(8,128)(2,1)S(1)} all-gather(bf16[32,1,3328]{2,0,1:T(8,128)(2,1)S(1)} %slice.9), channel_id=3, replica_groups=mesh['zh'=8,'zl'=4,'a'=4,'tp'=8] {'a'}, dimensions={0}, use_global_device_ids=true | all-gather | bytes 1064960 | tf_op jit(solution)/shard_map/all_gather | solution.py:226
  101.6 0.0 all-to-all-done.2.sums
  101.6 0.0 copy-done
  101.6 0.0 copy-done.1
  101.6 2.2 %third.1 = (f32[1,3328]{1,0:T(1,128)}, f32[8,3328]{1,0:T(8,128)}, bf16[1,3328]{1,0:T(2,128)(2,1)}, bf16[128,3328]{1,0:T(8,128)(2,1)}) custom-call(f32[8,88,128]{2,1,0:T(8,128)S(1)} %all-to-all-done.2.sums, bf16[128,3456]{1,0:T(8,128)(2,1)S(1)} %bitcast.10, bf16[128,3328]{1,0:T(8,128)(2,1)S(1)} %bitcast.11, f32[1,3328]{1,0:T(1,128)S(1)} %copy-done, ...), custom_call_target="tpu_custom_call" | custom-call | tf_op jit(solution)/shard_map/third/pallas_call | solution.py:201
  (6 shorter events, 0.1 us)
Async XLA Ops:
  84.2 6.5 %copy-start.2 = (bf16[128,128]{1,0:T(8,128)(2,1)S(1)}, bf16[128,128]{1,0:T(8,128)(2,1)}, u32[]{:S(2)}) copy-start(bf16[128,128]{1,0:T(8,128)(2,1)} %param.9) | copy-start | bytes 98308
  84.2 17.4 %all-to-all-start.2 = ((f32[8,88,128]{2,1,0:T(8,128)}), f32[8,88,128]{2,1,0:T(8,128)S(1)}, u32[]{:S(2)}, u32[]{:S(2)}) async-start(f32[8,88,128]{2,1,0:T(8,128)} %second.1), calls=%async_computation.2 | async-start | bytes 720896 | tf_op jit(solution)/shard_map/all_to_all | solution.py:22
  90.9 10.7 %copy-start = (f32[1,3328]{1,0:T(1,128)S(1)}, f32[1,3328]{1,0:T(1,128)}, u32[]{:S(2)}) copy-start(f32[1,3328]{1,0:T(1,128)} %momentum.1) | copy-start | bytes 39940
  90.9 10.7 %copy-start.1 = (f32[1,3328]{1,0:T(1,128)S(1)}, f32[1,3328]{1,0:T(1,128)}, u32[]{:S(2)}) copy-start(f32[1,3328]{1,0:T(1,128)} %gradient.1) | copy-start | bytes 39940
